TPU v7x, 32 devices: a whole 2x2x4 slice. The times are simulated.
32 devices in a mesh: sub: 16 (over z, y, x), freq: 2 (over core).
Axes of the slice: x: 2, y: 2, z: 4, core: 2. Of those that a mesh axis runs over, the one named last changes fastest.
Arguments:
- facet_image: bfloat16 [2, 1024, 1024], P('freq', 'sub'), may hold values from -0.015625 to 0.015625
- facet_tile: int32 [2, 2], P('freq'), may hold values from 0 to 63
- subgrid_cell: int32 [16, 2], P('sub'), may hold values from 0 to 65535
- row_subgrid: int32 [32768], P(('sub', 'freq')), may hold values from 0 to 15, as said below
- row_uv: float32 [2, 32768], P(None, ('sub', 'freq')), may hold values from 0 to 256
- observed: float32 [2, 32768], P(None, ('sub', 'freq')), may hold values from -6 to 6
Outputs:
- residual_vis: float32 [2, 32768], P(None, ('sub', 'freq'))
Inputs may be any that keep to these rules, and one draw needn't show every extreme that they name: `row_subgrid`: the subgrid whose cells hold the row's visibility; the rows of one device's block (aligned blocks of 1024 rows) name exactly 8 cyclically consecutive subgrids c, c + 1, ..., c + 8 - 1 (mod 16).
All inputs are finite; a program needn't handle non-finite values.
Results may differ from a plain program's by a relative error of at most 0.0035.
Values may be sent and summed in bfloat16 or wider, within the bound.
A program may use at most 64 MiB of HBM per device.

v0:
```python
import math

import jax
import jax.numpy as jnp
from jax import lax
from jax.sharding import PartitionSpec as P

SG = 256
FACET = 1024
NIMG = 65536


TWO_PI = 2.0 * math.pi


def from_behind(shard, axis, by):
    size = lax.axis_size(axis)
    return lax.ppermute(shard, axis, [(i, (i + by) % size) for i in range(size)])


def facet_window(count):
    position = (2.0 * jnp.arange(count, dtype=jnp.float32) + 1.0) / count - 1.0
    return 1.0 - 0.75 * position * position


def grid_taper(count):
    position = (2.0 * jnp.arange(count, dtype=jnp.float32) + 1.0) / count - 1.0
    return 1.0 - 0.5 * position * position


def phase_table(first_cells, second_cells, weights):
    product = first_cells[:, None] * second_cells[None, :] % NIMG
    angle = TWO_PI / NIMG * product.astype(jnp.float32)
    real_part = (weights * jnp.cos(angle)).astype(jnp.bfloat16)
    imag_part = (-weights * jnp.sin(angle)).astype(jnp.bfloat16)
    return (real_part, imag_part)


def plain_dot(left, right):
    return jnp.dot(left, right, preferred_element_type=jnp.float32)


def dot_trans(left, right):
    return lax.dot_general(
        left, right, (((1,), (1,)), ((), ())), preferred_element_type=jnp.float32
    )


def kernel_tables():
    spots = jnp.arange(SG, dtype=jnp.int32)
    angle = TWO_PI / SG * (spots[:, None] * spots[None, :] % SG).astype(jnp.float32)
    return (jnp.cos(angle).astype(jnp.bfloat16), jnp.sin(angle).astype(jnp.bfloat16))


def half_transform(grid_real, grid_imag, kernel_real, kernel_imag):
    kernel_both = jnp.concatenate([kernel_real, kernel_imag], axis=1)
    first_real = plain_dot(grid_real, kernel_both)
    first_imag = plain_dot(grid_imag, kernel_both)
    half_real = (first_real[:, :SG] - first_imag[:, SG:]).astype(jnp.bfloat16)
    half_imag = (first_real[:, SG:] + first_imag[:, :SG]).astype(jnp.bfloat16)
    return jnp.concatenate([half_real, half_imag], axis=1)


def image_from_half(half_both, kernel_real, kernel_imag):
    second_real = plain_dot(kernel_real, half_both)
    second_imag = plain_dot(kernel_imag, half_both)
    taper = grid_taper(SG)
    scale = taper[:, None] * taper[None, :] / (SG * SG)
    image_real = ((second_real[:, :SG] - second_imag[:, SG:]) * scale).astype(jnp.bfloat16)
    image_imag = ((second_real[:, SG:] + second_imag[:, :SG]) * scale).astype(jnp.bfloat16)
    return jnp.concatenate([image_real, image_imag], axis=0)


def degrid(image_both, match, u_pos, v_pos):
    spots = jnp.arange(SG, dtype=jnp.float32)
    angle_u = TWO_PI / SG * u_pos[:, None] * spots[None, :]
    along_real = jnp.cos(angle_u).astype(jnp.bfloat16)
    along_imag = (-jnp.sin(angle_u)).astype(jnp.bfloat16)
    first = dot_trans(along_real, image_both)
    second = dot_trans(along_imag, image_both)
    inner_real = first[:, :SG] - second[:, SG:]
    inner_imag = first[:, SG:] + second[:, :SG]
    angle_v = TWO_PI / SG * v_pos[:, None] * spots[None, :]
    cross_real = jnp.cos(angle_v)
    cross_imag = -jnp.sin(angle_v)
    vis_real = jnp.sum(inner_real * cross_real - inner_imag * cross_imag, axis=1)
    vis_imag = jnp.sum(inner_real * cross_imag + inner_imag * cross_real, axis=1)
    return jnp.where(match[None, :], jnp.stack([vis_real, vis_imag]), 0.0)


def local(facet_image, facet_tile, subgrid_cell, row_subgrid, row_uv, observed):
    owners = lax.axis_size("sub")
    owner_float = lax.axis_index("sub").astype(jnp.float32)
    facet_rows = facet_image[0]
    window = facet_window(FACET)
    cells = jnp.arange(FACET, dtype=jnp.int32)
    spots = jnp.arange(SG, dtype=jnp.int32)
    x_cells = facet_tile[0, 0] * FACET + cells
    y_cells = facet_tile[0, 1] * FACET + cells
    col_real, col_imag = phase_table(x_cells, subgrid_cell[0, 0] + spots, window[:, None])
    col_both = jnp.concatenate([col_real, col_imag], axis=1)
    spectra = plain_dot(lax.all_gather(facet_rows, "sub", axis=0, tiled=True), col_both).astype(
        jnp.bfloat16
    )
    row_real, row_imag = phase_table(subgrid_cell[0, 1] + spots, y_cells, window[None, :])
    first = plain_dot(row_real, spectra)
    second = plain_dot(row_imag, spectra)
    term_real = first[:, :SG] - second[:, SG:]
    term_imag = first[:, SG:] + second[:, :SG]
    kernel_real, kernel_imag = kernel_tables()
    grid_real, grid_imag = lax.psum((term_real, term_imag), "freq")
    half_both = half_transform(
        grid_real.astype(jnp.bfloat16), grid_imag.astype(jnp.bfloat16), kernel_real, kernel_imag
    )
    image_both = image_from_half(half_both, kernel_real, kernel_imag)
    rows = row_subgrid.shape[0]

    def visit(block):
        match = block[0] == owner_float
        return lax.cond(
            jnp.any(match),
            lambda: degrid(image_both, match, block[1], block[2]),
            lambda: jnp.zeros((2, rows), jnp.float32),
        )

    def with_visit(block):
        return block.at[3:].add(visit(block))

    meta = jnp.concatenate([row_subgrid.astype(jnp.float32)[None, :], row_uv], axis=0)
    start_block = jnp.concatenate([meta, jnp.zeros((2, rows), jnp.float32)], axis=0)

    def turn_one(turn_index, block):
        return from_behind(with_visit(block), "sub", 1)

    finished = lax.fori_loop(0, owners, turn_one, start_block)
    predicted = finished[3:]
    return observed - predicted


def solution(mesh):
    placed = (
        P("freq", "sub", None),
        P("freq", None),
        P("sub", None),
        P(("sub", "freq")),
        P(None, ("sub", "freq")),
        P(None, ("sub", "freq")),
    )
    return jax.shard_map(
        local, mesh=mesh, in_specs=placed, out_specs=P(None, ("sub", "freq")), check_vma=False
    )
```

profile of v0, /device:TPU:8, one launch (start us, length us, event | category | flops | bytes accessed | tf_op | source)
XLA Modules:
  0.0 416.0 jit_solution(13842328959682900408)
XLA Ops:
  15.1 4.7 %multiply_convert_fusion.2 = (bf16[1024,256]{1,0:T(8,128)(2,1)S(1)}, bf16[1024,256]{1,0:T(8,128)(2,1)S(1)}) fusion(s32[256]{0:T(256)S(1)} %iota_add_fusion.2, s32[1024]{0:T(1024)S(1)} %iota_add_fusion, f32[1024]{0:T(1024)S(1)} %get-tuple-element.116, f32[1024]{0:T(1024)S(1)} %get-tuple-element.117), kind=kLoop, calls=%fused_computation.43 | loop fusion | flops 4718592 | bytes 1061888 | tf_op jit(solution)/shard_map/convert_element_type | solution.py:34
  19.9 52.2 %all-gather.3.cloned.1.call-done = bf16[1,1024,1024]{2,1,0:T(8,128)(2,1)} async-done(((bf16[1,64,1024]{2,1,0:T(8,128)(2,1)}), bf16[1,1024,1024]{2,1,0:T(8,128)(2,1)}) %all-gather.3.cloned.1.call-update) | async-done | bytes 2097168 | tf_op jit(solution)/shard_map/all_gather | solution.py:102
  83.2 5.0 %all-reduce.2 = (bf16[256,256]{1,0:T(8,128)(2,1)S(1)}, bf16[256,256]{1,0:T(8,128)(2,1)S(1)}) all-reduce(f32[256,256]{1,0:T(8,128)S(1)} %get-tuple-element.109, f32[256,256]{1,0:T(8,128)S(1)} %get-tuple-element.108), channel_id=1, replica_groups=mesh['sub'=16,'freq'=2] {'freq'}, use_global_device_ids=true, to_apply=%region_1.2 | all-reduce | flops 131072 | bytes 786432 | tf_op jit(solution)/shard_map/psum | solution.py:111
  91.2 317.4 %while.13 = (s32[]{:T(128)}, f32[5,1024]{1,0:T(8,128)S(1)}, f32[]{:T(128)}, bf16[512,256]{1,0:T(8,128)(2,1)S(1)}, s32[]{:T(128)}, /*index=5*/s32[]{:T(128)}, s32[]{:T(128)}) while((s32[]{:T(128)}, f32[5,1024]{1,0:T(8,128)S(1)}, f32[]{:T(128)}, bf16[512,256]{1,0:T(8,128)(2,1)S(1)}, s32[]{:T(128)}, /*index=5*/s32[]{:T(128)}, s32[]{:T(128)}) %tuple.53), condition=%wide.region_8.9_spmd, body=%wide.region_2.8_spmd.sunk | while | flops 541335552 | bytes 9138340 | solution.py:135
  92.7 15.0 %collective-permute-start = (f32[5,1024]{1,0:T(8,128)S(1)}, f32[5,1024]{1,0:T(8,128)S(1)}, u32[]{:S(2)}, u32[]{:S(2)}) collective-permute-start(f32[5,1024]{1,0:T(8,128)S(1)} %scatter-add.6), channel_id=1, source_target_pairs={{0,2},{2,4},{4,6},{6,8},{8,10},{10,12},{12,14},{14,16},{16,18},{18... | collective-permute-start | bytes 61448 | tf_op jit(solution)/shard_map/while/body/eval_jaxpr/ppermute | solution.py:18
  110.7 16.1 %collective-permute-start = (f32[5,1024]{1,0:T(8,128)S(1)}, f32[5,1024]{1,0:T(8,128)S(1)}, u32[]{:S(2)}, u32[]{:S(2)}) collective-permute-start(f32[5,1024]{1,0:T(8,128)S(1)} %scatter-add.6), channel_id=1, source_target_pairs={{0,2},{2,4},{4,6},{6,8},{8,10},{10,12},{12,14},{14,16},{16,18},{18... | collective-permute-start | bytes 61448 | tf_op jit(solution)/shard_map/while/body/eval_jaxpr/ppermute | solution.py:18
  136.9 13.7 %conditional.2 = (f32[2,1024]{1,0:T(2,128)S(1)}) conditional(s32[]{:T(128)} %convert_element_type.144, () %tuple.51, (pred[1,1024]{1,0:T(4,128)(4,1)S(1)}, f32[5,1024]{1,0:T(8,128)S(1)}, bf16[512,256]{1,0:T(8,128)(2,1)S(1)}) %tuple.52), branch_computations={%region_4.4_spmd, %region_5.7_spmd} | conditional | flops 541331456 | bytes 8969225 | solution.py:120
  141.4 4.7 %fusion.2 = f32[1024,512]{0,1:T(8,128)S(1)} fusion(bf16[512,256]{1,0:T(8,128)(2,1)S(1)} %get-tuple-element.79, f32[1024]{0:T(1024)S(1)} %bitcast.21), kind=kOutput, calls=%fused_computation.11 | convolution fusion | flops 269221888 | bytes 2363392 | tf_op jit(solution)/shard_map/while/body/eval_jaxpr/cond/branch_1_fun/dot_general | solution.py:44
  152.6 12.0 %collective-permute-done = f32[5,1024]{1,0:T(8,128)S(1)} collective-permute-done((f32[5,1024]{1,0:T(8,128)S(1)}, f32[5,1024]{1,0:T(8,128)S(1)}, u32[]{:S(2)}, u32[]{:S(2)}) %collective-permute-start) | collective-permute-done | bytes 20512 | tf_op jit(solution)/shard_map/while/body/eval_jaxpr/ppermute | solution.py:18
  165.8 13.7 %conditional.2 = (f32[2,1024]{1,0:T(2,128)S(1)}) conditional(s32[]{:T(128)} %convert_element_type.144, () %tuple.51, (pred[1,1024]{1,0:T(4,128)(4,1)S(1)}, f32[5,1024]{1,0:T(8,128)S(1)}, bf16[512,256]{1,0:T(8,128)(2,1)S(1)}) %tuple.52), branch_computations={%region_4.4_spmd, %region_5.7_spmd} | conditional | flops 541331456 | bytes 8969225 | solution.py:120
  170.3 4.7 %fusion.2 = f32[1024,512]{0,1:T(8,128)S(1)} fusion(bf16[512,256]{1,0:T(8,128)(2,1)S(1)} %get-tuple-element.79, f32[1024]{0:T(1024)S(1)} %bitcast.21), kind=kOutput, calls=%fused_computation.11 | convolution fusion | flops 269221888 | bytes 2363392 | tf_op jit(solution)/shard_map/while/body/eval_jaxpr/cond/branch_1_fun/dot_general | solution.py:44
  179.8 5.7 %collective-permute-done = f32[5,1024]{1,0:T(8,128)S(1)} collective-permute-done((f32[5,1024]{1,0:T(8,128)S(1)}, f32[5,1024]{1,0:T(8,128)S(1)}, u32[]{:S(2)}, u32[]{:S(2)}) %collective-permute-start) | collective-permute-done | bytes 20512 | tf_op jit(solution)/shard_map/while/body/eval_jaxpr/ppermute | solution.py:18
  187.0 15.6 %collective-permute-start = (f32[5,1024]{1,0:T(8,128)S(1)}, f32[5,1024]{1,0:T(8,128)S(1)}, u32[]{:S(2)}, u32[]{:S(2)}) collective-permute-start(f32[5,1024]{1,0:T(8,128)S(1)} %scatter-add.6), channel_id=1, source_target_pairs={{0,2},{2,4},{4,6},{6,8},{8,10},{10,12},{12,14},{14,16},{16,18},{18... | collective-permute-start | bytes 61448 | tf_op jit(solution)/shard_map/while/body/eval_jaxpr/ppermute | solution.py:18
  205.3 13.7 %conditional.2 = (f32[2,1024]{1,0:T(2,128)S(1)}) conditional(s32[]{:T(128)} %convert_element_type.144, () %tuple.51, (pred[1,1024]{1,0:T(4,128)(4,1)S(1)}, f32[5,1024]{1,0:T(8,128)S(1)}, bf16[512,256]{1,0:T(8,128)(2,1)S(1)}) %tuple.52), branch_computations={%region_4.4_spmd, %region_5.7_spmd} | conditional | flops 541331456 | bytes 8969225 | solution.py:120
  209.9 4.7 %fusion.2 = f32[1024,512]{0,1:T(8,128)S(1)} fusion(bf16[512,256]{1,0:T(8,128)(2,1)S(1)} %get-tuple-element.79, f32[1024]{0:T(1024)S(1)} %bitcast.21), kind=kOutput, calls=%fused_computation.11 | convolution fusion | flops 269221888 | bytes 2363392 | tf_op jit(solution)/shard_map/while/body/eval_jaxpr/cond/branch_1_fun/dot_general | solution.py:44
  219.4 5.7 %collective-permute-done = f32[5,1024]{1,0:T(8,128)S(1)} collective-permute-done((f32[5,1024]{1,0:T(8,128)S(1)}, f32[5,1024]{1,0:T(8,128)S(1)}, u32[]{:S(2)}, u32[]{:S(2)}) %collective-permute-start) | collective-permute-done | bytes 20512 | tf_op jit(solution)/shard_map/while/body/eval_jaxpr/ppermute | solution.py:18
  226.3 13.7 %conditional.2 = (f32[2,1024]{1,0:T(2,128)S(1)}) conditional(s32[]{:T(128)} %convert_element_type.144, () %tuple.51, (pred[1,1024]{1,0:T(4,128)(4,1)S(1)}, f32[5,1024]{1,0:T(8,128)S(1)}, bf16[512,256]{1,0:T(8,128)(2,1)S(1)}) %tuple.52), branch_computations={%region_4.4_spmd, %region_5.7_spmd} | conditional | flops 541331456 | bytes 8969225 | solution.py:120
  247.2 13.7 %conditional.2 = (f32[2,1024]{1,0:T(2,128)S(1)}) conditional(s32[]{:T(128)} %convert_element_type.144, () %tuple.51, (pred[1,1024]{1,0:T(4,128)(4,1)S(1)}, f32[5,1024]{1,0:T(8,128)S(1)}, bf16[512,256]{1,0:T(8,128)(2,1)S(1)}) %tuple.52), branch_computations={%region_4.4_spmd, %region_5.7_spmd} | conditional | flops 541331456 | bytes 8969225 | solution.py:120
  251.8 4.7 %fusion.2 = f32[1024,512]{0,1:T(8,128)S(1)} fusion(bf16[512,256]{1,0:T(8,128)(2,1)S(1)} %get-tuple-element.79, f32[1024]{0:T(1024)S(1)} %bitcast.21), kind=kOutput, calls=%fused_computation.11 | convolution fusion | flops 269221888 | bytes 2363392 | tf_op jit(solution)/shard_map/while/body/eval_jaxpr/cond/branch_1_fun/dot_general | solution.py:44
  268.4 13.7 %conditional.2 = (f32[2,1024]{1,0:T(2,128)S(1)}) conditional(s32[]{:T(128)} %convert_element_type.144, () %tuple.51, (pred[1,1024]{1,0:T(4,128)(4,1)S(1)}, f32[5,1024]{1,0:T(8,128)S(1)}, bf16[512,256]{1,0:T(8,128)(2,1)S(1)}) %tuple.52), branch_computations={%region_4.4_spmd, %region_5.7_spmd} | conditional | flops 541331456 | bytes 8969225 | solution.py:120
  273.0 4.7 %fusion.2 = f32[1024,512]{0,1:T(8,128)S(1)} fusion(bf16[512,256]{1,0:T(8,128)(2,1)S(1)} %get-tuple-element.79, f32[1024]{0:T(1024)S(1)} %bitcast.21), kind=kOutput, calls=%fused_computation.11 | convolution fusion | flops 269221888 | bytes 2363392 | tf_op jit(solution)/shard_map/while/body/eval_jaxpr/cond/branch_1_fun/dot_general | solution.py:44
  289.3 13.7 %conditional.2 = (f32[2,1024]{1,0:T(2,128)S(1)}) conditional(s32[]{:T(128)} %convert_element_type.144, () %tuple.51, (pred[1,1024]{1,0:T(4,128)(4,1)S(1)}, f32[5,1024]{1,0:T(8,128)S(1)}, bf16[512,256]{1,0:T(8,128)(2,1)S(1)}) %tuple.52), branch_computations={%region_4.4_spmd, %region_5.7_spmd} | conditional | flops 541331456 | bytes 8969225 | solution.py:120
  310.5 16.7 %collective-permute-start = (f32[5,1024]{1,0:T(8,128)S(1)}, f32[5,1024]{1,0:T(8,128)S(1)}, u32[]{:S(2)}, u32[]{:S(2)}) collective-permute-start(f32[5,1024]{1,0:T(8,128)S(1)} %scatter-add.6), channel_id=1, source_target_pairs={{0,2},{2,4},{4,6},{6,8},{8,10},{10,12},{12,14},{14,16},{16,18},{18... | collective-permute-start | bytes 61448 | tf_op jit(solution)/shard_map/while/body/eval_jaxpr/ppermute | solution.py:18
  330.1 13.7 %conditional.2 = (f32[2,1024]{1,0:T(2,128)S(1)}) conditional(s32[]{:T(128)} %convert_element_type.144, () %tuple.51, (pred[1,1024]{1,0:T(4,128)(4,1)S(1)}, f32[5,1024]{1,0:T(8,128)S(1)}, bf16[512,256]{1,0:T(8,128)(2,1)S(1)}) %tuple.52), branch_computations={%region_4.4_spmd, %region_5.7_spmd} | conditional | flops 541331456 | bytes 8969225 | solution.py:120
  334.7 4.7 %fusion.2 = f32[1024,512]{0,1:T(8,128)S(1)} fusion(bf16[512,256]{1,0:T(8,128)(2,1)S(1)} %get-tuple-element.79, f32[1024]{0:T(1024)S(1)} %bitcast.21), kind=kOutput, calls=%fused_computation.11 | convolution fusion | flops 269221888 | bytes 2363392 | tf_op jit(solution)/shard_map/while/body/eval_jaxpr/cond/branch_1_fun/dot_general | solution.py:44
  344.1 5.7 %collective-permute-done = f32[5,1024]{1,0:T(8,128)S(1)} collective-permute-done((f32[5,1024]{1,0:T(8,128)S(1)}, f32[5,1024]{1,0:T(8,128)S(1)}, u32[]{:S(2)}, u32[]{:S(2)}) %collective-permute-start) | collective-permute-done | bytes 20512 | tf_op jit(solution)/shard_map/while/body/eval_jaxpr/ppermute | solution.py:18
  351.0 13.7 %conditional.2 = (f32[2,1024]{1,0:T(2,128)S(1)}) conditional(s32[]{:T(128)} %convert_element_type.144, () %tuple.51, (pred[1,1024]{1,0:T(4,128)(4,1)S(1)}, f32[5,1024]{1,0:T(8,128)S(1)}, bf16[512,256]{1,0:T(8,128)(2,1)S(1)}) %tuple.52), branch_computations={%region_4.4_spmd, %region_5.7_spmd} | conditional | flops 541331456 | bytes 8969225 | solution.py:120
  365.1 5.7 %collective-permute-done = f32[5,1024]{1,0:T(8,128)S(1)} collective-permute-done((f32[5,1024]{1,0:T(8,128)S(1)}, f32[5,1024]{1,0:T(8,128)S(1)}, u32[]{:S(2)}, u32[]{:S(2)}) %collective-permute-start) | collective-permute-done | bytes 20512 | tf_op jit(solution)/shard_map/while/body/eval_jaxpr/ppermute | solution.py:18
  372.2 12.0 %collective-permute-start = (f32[5,1024]{1,0:T(8,128)S(1)}, f32[5,1024]{1,0:T(8,128)S(1)}, u32[]{:S(2)}, u32[]{:S(2)}) collective-permute-start(f32[5,1024]{1,0:T(8,128)S(1)} %scatter-add.6), channel_id=1, source_target_pairs={{0,2},{2,4},{4,6},{6,8},{8,10},{10,12},{12,14},{14,16},{16,18},{18... | collective-permute-start | bytes 61448 | tf_op jit(solution)/shard_map/while/body/eval_jaxpr/ppermute | solution.py:18
  388.8 13.7 %conditional.2 = (f32[2,1024]{1,0:T(2,128)S(1)}) conditional(s32[]{:T(128)} %convert_element_type.144, () %tuple.51, (pred[1,1024]{1,0:T(4,128)(4,1)S(1)}, f32[5,1024]{1,0:T(8,128)S(1)}, bf16[512,256]{1,0:T(8,128)(2,1)S(1)}) %tuple.52), branch_computations={%region_4.4_spmd, %region_5.7_spmd} | conditional | flops 541331456 | bytes 8969225 | solution.py:120
  393.4 4.7 %fusion.2 = f32[1024,512]{0,1:T(8,128)S(1)} fusion(bf16[512,256]{1,0:T(8,128)(2,1)S(1)} %get-tuple-element.79, f32[1024]{0:T(1024)S(1)} %bitcast.21), kind=kOutput, calls=%fused_computation.11 | convolution fusion | flops 269221888 | bytes 2363392 | tf_op jit(solution)/shard_map/while/body/eval_jaxpr/cond/branch_1_fun/dot_general | solution.py:44
  402.8 5.7 %collective-permute-done = f32[5,1024]{1,0:T(8,128)S(1)} collective-permute-done((f32[5,1024]{1,0:T(8,128)S(1)}, f32[5,1024]{1,0:T(8,128)S(1)}, u32[]{:S(2)}, u32[]{:S(2)}) %collective-permute-start) | collective-permute-done | bytes 20512 | tf_op jit(solution)/shard_map/while/body/eval_jaxpr/ppermute | solution.py:18
  (179 shorter events, 180.8 us)
Async XLA Ops:
  6.5 65.5 %all-gather.3.cloned.1.call-start = ((), (), s32[]{:S(2)}) async-start(), calls=%async_computation | async-start | bytes 2228224 | tf_op jit(solution)/shard_map/all_gather | solution.py:102
  91.2 317.4 %copy-start = (f32[2,1024]{1,0:T(2,128)S(1)}, f32[2,1024]{1,0:T(2,128)}, u32[]{:S(2)}) copy-start(f32[2,1024]{1,0:T(2,128)} %param.17) | copy-start | bytes 24580
  92.7 16.6 %collective-permute-start = (f32[5,1024]{1,0:T(8,128)S(1)}, f32[5,1024]{1,0:T(8,128)S(1)}, u32[]{:S(2)}, u32[]{:S(2)}) collective-permute-start(f32[5,1024]{1,0:T(8,128)S(1)} %scatter-add.6), channel_id=1, source_target_pairs={{0,2},{2,4},{4,6},{6,8},{8,10},{10,12},{12,14},{14,16},{16,18},{18... | collective-permute-start | bytes 61448 | tf_op jit(solution)/shard_map/while/body/eval_jaxpr/ppermute | solution.py:18
  110.7 17.7 %collective-permute-start = (f32[5,1024]{1,0:T(8,128)S(1)}, f32[5,1024]{1,0:T(8,128)S(1)}, u32[]{:S(2)}, u32[]{:S(2)}) collective-permute-start(f32[5,1024]{1,0:T(8,128)S(1)} %scatter-add.6), channel_id=1, source_target_pairs={{0,2},{2,4},{4,6},{6,8},{8,10},{10,12},{12,14},{14,16},{16,18},{18... | collective-permute-start | bytes 61448 | tf_op jit(solution)/shard_map/while/body/eval_jaxpr/ppermute | solution.py:18
  129.9 5.8 %collective-permute-start = (f32[5,1024]{1,0:T(8,128)S(1)}, f32[5,1024]{1,0:T(8,128)S(1)}, u32[]{:S(2)}, u32[]{:S(2)}) collective-permute-start(f32[5,1024]{1,0:T(8,128)S(1)} %scatter-add.6), channel_id=1, source_target_pairs={{0,2},{2,4},{4,6},{6,8},{8,10},{10,12},{12,14},{14,16},{16,18},{18... | collective-permute-start | bytes 61448 | tf_op jit(solution)/shard_map/while/body/eval_jaxpr/ppermute | solution.py:18
  150.8 13.7 %collective-permute-start = (f32[5,1024]{1,0:T(8,128)S(1)}, f32[5,1024]{1,0:T(8,128)S(1)}, u32[]{:S(2)}, u32[]{:S(2)}) collective-permute-start(f32[5,1024]{1,0:T(8,128)S(1)} %scatter-add.6), channel_id=1, source_target_pairs={{0,2},{2,4},{4,6},{6,8},{8,10},{10,12},{12,14},{14,16},{16,18},{18... | collective-permute-start | bytes 61448 | tf_op jit(solution)/shard_map/while/body/eval_jaxpr/ppermute | solution.py:18
  179.7 5.8 %collective-permute-start = (f32[5,1024]{1,0:T(8,128)S(1)}, f32[5,1024]{1,0:T(8,128)S(1)}, u32[]{:S(2)}, u32[]{:S(2)}) collective-permute-start(f32[5,1024]{1,0:T(8,128)S(1)} %scatter-add.6), channel_id=1, source_target_pairs={{0,2},{2,4},{4,6},{6,8},{8,10},{10,12},{12,14},{14,16},{16,18},{18... | collective-permute-start | bytes 61448 | tf_op jit(solution)/shard_map/while/body/eval_jaxpr/ppermute | solution.py:18
  187.0 17.1 %collective-permute-start = (f32[5,1024]{1,0:T(8,128)S(1)}, f32[5,1024]{1,0:T(8,128)S(1)}, u32[]{:S(2)}, u32[]{:S(2)}) collective-permute-start(f32[5,1024]{1,0:T(8,128)S(1)} %scatter-add.6), channel_id=1, source_target_pairs={{0,2},{2,4},{4,6},{6,8},{8,10},{10,12},{12,14},{14,16},{16,18},{18... | collective-permute-start | bytes 61448 | tf_op jit(solution)/shard_map/while/body/eval_jaxpr/ppermute | solution.py:18
  219.3 5.8 %collective-permute-start = (f32[5,1024]{1,0:T(8,128)S(1)}, f32[5,1024]{1,0:T(8,128)S(1)}, u32[]{:S(2)}, u32[]{:S(2)}) collective-permute-start(f32[5,1024]{1,0:T(8,128)S(1)} %scatter-add.6), channel_id=1, source_target_pairs={{0,2},{2,4},{4,6},{6,8},{8,10},{10,12},{12,14},{14,16},{16,18},{18... | collective-permute-start | bytes 61448 | tf_op jit(solution)/shard_map/while/body/eval_jaxpr/ppermute | solution.py:18
  240.2 5.8 %collective-permute-start = (f32[5,1024]{1,0:T(8,128)S(1)}, f32[5,1024]{1,0:T(8,128)S(1)}, u32[]{:S(2)}, u32[]{:S(2)}) collective-permute-start(f32[5,1024]{1,0:T(8,128)S(1)} %scatter-add.6), channel_id=1, source_target_pairs={{0,2},{2,4},{4,6},{6,8},{8,10},{10,12},{12,14},{14,16},{16,18},{18... | collective-permute-start | bytes 61448 | tf_op jit(solution)/shard_map/while/body/eval_jaxpr/ppermute | solution.py:18
  261.2 6.0 %collective-permute-start = (f32[5,1024]{1,0:T(8,128)S(1)}, f32[5,1024]{1,0:T(8,128)S(1)}, u32[]{:S(2)}, u32[]{:S(2)}) collective-permute-start(f32[5,1024]{1,0:T(8,128)S(1)} %scatter-add.6), channel_id=1, source_target_pairs={{0,2},{2,4},{4,6},{6,8},{8,10},{10,12},{12,14},{14,16},{16,18},{18... | collective-permute-start | bytes 61448 | tf_op jit(solution)/shard_map/while/body/eval_jaxpr/ppermute | solution.py:18
  282.4 5.8 %collective-permute-start = (f32[5,1024]{1,0:T(8,128)S(1)}, f32[5,1024]{1,0:T(8,128)S(1)}, u32[]{:S(2)}, u32[]{:S(2)}) collective-permute-start(f32[5,1024]{1,0:T(8,128)S(1)} %scatter-add.6), channel_id=1, source_target_pairs={{0,2},{2,4},{4,6},{6,8},{8,10},{10,12},{12,14},{14,16},{16,18},{18... | collective-permute-start | bytes 61448 | tf_op jit(solution)/shard_map/while/body/eval_jaxpr/ppermute | solution.py:18
  303.3 5.8 %collective-permute-start = (f32[5,1024]{1,0:T(8,128)S(1)}, f32[5,1024]{1,0:T(8,128)S(1)}, u32[]{:S(2)}, u32[]{:S(2)}) collective-permute-start(f32[5,1024]{1,0:T(8,128)S(1)} %scatter-add.6), channel_id=1, source_target_pairs={{0,2},{2,4},{4,6},{6,8},{8,10},{10,12},{12,14},{14,16},{16,18},{18... | collective-permute-start | bytes 61448 | tf_op jit(solution)/shard_map/while/body/eval_jaxpr/ppermute | solution.py:18
  310.5 18.3 %collective-permute-start = (f32[5,1024]{1,0:T(8,128)S(1)}, f32[5,1024]{1,0:T(8,128)S(1)}, u32[]{:S(2)}, u32[]{:S(2)}) collective-permute-start(f32[5,1024]{1,0:T(8,128)S(1)} %scatter-add.6), channel_id=1, source_target_pairs={{0,2},{2,4},{4,6},{6,8},{8,10},{10,12},{12,14},{14,16},{16,18},{18... | collective-permute-start | bytes 61448 | tf_op jit(solution)/shard_map/while/body/eval_jaxpr/ppermute | solution.py:18
  344.1 5.8 %collective-permute-start = (f32[5,1024]{1,0:T(8,128)S(1)}, f32[5,1024]{1,0:T(8,128)S(1)}, u32[]{:S(2)}, u32[]{:S(2)}) collective-permute-start(f32[5,1024]{1,0:T(8,128)S(1)} %scatter-add.6), channel_id=1, source_target_pairs={{0,2},{2,4},{4,6},{6,8},{8,10},{10,12},{12,14},{14,16},{16,18},{18... | collective-permute-start | bytes 61448 | tf_op jit(solution)/shard_map/while/body/eval_jaxpr/ppermute | solution.py:18
  365.0 5.8 %collective-permute-start = (f32[5,1024]{1,0:T(8,128)S(1)}, f32[5,1024]{1,0:T(8,128)S(1)}, u32[]{:S(2)}, u32[]{:S(2)}) collective-permute-start(f32[5,1024]{1,0:T(8,128)S(1)} %scatter-add.6), channel_id=1, source_target_pairs={{0,2},{2,4},{4,6},{6,8},{8,10},{10,12},{12,14},{14,16},{16,18},{18... | collective-permute-start | bytes 61448 | tf_op jit(solution)/shard_map/while/body/eval_jaxpr/ppermute | solution.py:18
  372.2 15.4 %collective-permute-start = (f32[5,1024]{1,0:T(8,128)S(1)}, f32[5,1024]{1,0:T(8,128)S(1)}, u32[]{:S(2)}, u32[]{:S(2)}) collective-permute-start(f32[5,1024]{1,0:T(8,128)S(1)} %scatter-add.6), channel_id=1, source_target_pairs={{0,2},{2,4},{4,6},{6,8},{8,10},{10,12},{12,14},{14,16},{16,18},{18... | collective-permute-start | bytes 61448 | tf_op jit(solution)/shard_map/while/body/eval_jaxpr/ppermute | solution.py:18
  402.8 5.8 %collective-permute-start = (f32[5,1024]{1,0:T(8,128)S(1)}, f32[5,1024]{1,0:T(8,128)S(1)}, u32[]{:S(2)}, u32[]{:S(2)}) collective-permute-start(f32[5,1024]{1,0:T(8,128)S(1)} %scatter-add.6), channel_id=1, source_target_pairs={{0,2},{2,4},{4,6},{6,8},{8,10},{10,12},{12,14},{14,16},{16,18},{18... | collective-permute-start | bytes 61448 | tf_op jit(solution)/shard_map/while/body/eval_jaxpr/ppermute | solution.py:18
Sparse Core Ops, SparseCore 0:
  10.1 61.9 all-gather.2
where the time goes:
time: 416 us
  waiting for transfers between devices  114 us (27%)
  matrix products  106 us (25%)
  starting transfers between devices  95.3 us (23%)
  other arithmetic  64.5 us (16%)
  between operations  14.7 us (4%)
  loops' own time  10.1 us (2%)
  local copies, waits for them, and re-layouts  6.22 us (1%)
  blocking collectives  5.02 us (1%)
    ppermute x16, starting transfers between devices, from_behind(): lax.ppermute(shard, axis, [(i, (i + by) % size) for i in range(size)])  95.3 us
    dot_general x20, matrix products, dot_trans(): lax.dot_general(left, right, (((1,), (1,)), ((), ())), preferred_element_...  92.1 us
    ppermute x16, waiting for transfers between devices, from_behind(): lax.ppermute(shard, axis, [(i, (i + by) % size) for i in range(size)])  61.4 us
    all_gather x1, waiting for transfers between devices, local(): lax.all_gather(facet_rows, 'sub', axis=0, tiled=True)  52.2 us
    reduce_sum x10, other arithmetic, degrid(): jnp.sum(inner_real * cross_real - inner_imag * cross_imag, axis=1)  44.1 us
    dot_general x7, matrix products, plain_dot(): return jnp.dot(left, right, preferred_element_type=jnp.float32)  13.7 us
    reduce_or x16, other arithmetic, visit(): jnp.any(match)  10.2 us
    another operation x1, loops' own time, local(): finished = lax.fori_loop(0, owners, turn_one, start_block)  9.46 us
  transfers between devices with their start and end apart: 17, of which 17 were waited for; matrix products, arithmetic and copies ran while one was open for 3% of the time, Pallas kernels for 0%

commit v1 on v0

v1 whole, which is shorter than its diff:
```python
import math

import numpy as np
import jax
import jax.numpy as jnp
from jax import lax
from jax.experimental import pallas as pl
from jax.experimental.pallas import tpu as pltpu
from jax.sharding import PartitionSpec as P

SG = 256
FACET = 1024
NIMG = 65536
CHUNK = 256
HALF_PI = math.pi / 2.0


def nt_dot(left, right):
    return lax.dot_general(
        left, right, (((1,), (1,)), ((), ())), preferred_element_type=jnp.float32
    )


def plain_dot(left, right):
    return jnp.dot(left, right, preferred_element_type=jnp.float32)


def unit_root(quarters):
    whole = jnp.floor(quarters + 0.5)
    angle = HALF_PI * (quarters - whole)
    turn = whole.astype(jnp.int32)
    sq = angle * angle
    sin_part = angle * (
        1.0 + sq * (-1.0 / 6.0 + sq * (1.0 / 120.0 + sq * (-1.0 / 5040.0 + sq * (1.0 / 362880.0))))
    )
    cos_part = 1.0 + sq * (
        -0.5 + sq * (1.0 / 24.0 + sq * (-1.0 / 720.0 + sq * (1.0 / 40320.0)))
    )
    odd = (turn & 1) == 1
    cos_turned = jnp.where(odd, sin_part, cos_part)
    sin_turned = jnp.where(odd, cos_part, sin_part)
    cos_out = jnp.where(((turn + 1) & 2) == 2, -cos_turned, cos_turned)
    sin_out = jnp.where((turn & 2) == 2, -sin_turned, sin_turned)
    return cos_out, -sin_out


def outer_product(coarse, fine):
    rows, lanes = coarse[0].shape
    cr, ci = coarse[0][:, None, :], coarse[1][:, None, :]
    fr, fi = fine[0][None, :, :], fine[1][None, :, :]
    real_part = (cr * fr - ci * fi).reshape(rows * 8, lanes)
    imag_part = (cr * fi + ci * fr).reshape(rows * 8, lanes)
    return real_part, imag_part


def window_table(first_cell, first_pixel):
    lanes = lax.broadcasted_iota(jnp.int32, (8, FACET), 1)
    fine_rows = lax.broadcasted_iota(jnp.int32, (8, FACET), 0)
    coarse_lanes = lax.broadcasted_iota(jnp.int32, (SG // 8, FACET), 1)
    coarse_rows = lax.broadcasted_iota(jnp.int32, (SG // 8, FACET), 0)
    position = (2.0 * lanes.astype(jnp.float32) + 1.0) / FACET - 1.0
    weights = 1.0 - 0.75 * position * position
    fine_phase = (fine_rows * (first_pixel + lanes)) & (NIMG - 1)
    coarse_phase = ((first_cell + 8 * coarse_rows) * (first_pixel + coarse_lanes)) & (NIMG - 1)
    fine = unit_root(fine_phase.astype(jnp.float32) * (4.0 / NIMG))
    coarse = unit_root(coarse_phase.astype(jnp.float32) * (4.0 / NIMG))
    real_part, imag_part = outer_product(coarse, (weights * fine[0], weights * fine[1]))
    return real_part.astype(jnp.bfloat16), imag_part.astype(jnp.bfloat16)


def facet_kernel(tile_ref, cell_ref, image_ref, out_ref, col_ref, spectra_ref):
    col_real, col_imag = window_table(cell_ref[0, 0], tile_ref[0, 0] * FACET)
    col_ref[:SG] = col_real
    col_ref[SG:] = col_imag
    for part in range(4):
        rows = slice(part * 256, part * 256 + 256)
        spectra_ref[:, rows] = nt_dot(col_ref[...], image_ref[rows]).astype(jnp.bfloat16)
    row_real, row_imag = window_table(cell_ref[0, 1], tile_ref[0, 1] * FACET)
    first = nt_dot(row_real, spectra_ref[...])
    second = nt_dot(row_imag, spectra_ref[...])
    out_ref[:, :SG] = first[:, :SG] - second[:, SG:]
    out_ref[:, SG:] = first[:, SG:] + second[:, :SG]


def subgrid_image(grid_real, grid_imag, kernel_real, kernel_imag):
    kernel_both = jnp.concatenate([kernel_real, kernel_imag], axis=1)
    first_real = plain_dot(grid_real, kernel_both)
    first_imag = plain_dot(grid_imag, kernel_both)
    half_real = (first_real[:, :SG] - first_imag[:, SG:]).astype(jnp.bfloat16)
    half_imag = (first_real[:, SG:] + first_imag[:, :SG]).astype(jnp.bfloat16)
    half_both = jnp.concatenate([half_real, half_imag], axis=1)
    second_real = plain_dot(kernel_real, half_both)
    second_imag = plain_dot(kernel_imag, half_both)

    def taper(axis):
        cells = lax.broadcasted_iota(jnp.int32, (SG, SG), axis).astype(jnp.float32)
        position = (2.0 * cells + 1.0) / SG - 1.0
        return 1.0 - 0.5 * position * position

    scale = taper(0) * taper(1) / (SG * SG)
    image_real = ((second_real[:, :SG] - second_imag[:, SG:]) * scale).astype(jnp.bfloat16)
    image_imag = ((second_real[:, SG:] + second_imag[:, :SG]) * scale).astype(jnp.bfloat16)
    return image_real, image_imag


def powers(position, lanes):
    quarters = position * (4.0 / SG)
    steps = lax.broadcasted_iota(jnp.int32, (8, lanes), 0).astype(jnp.float32)
    fine = unit_root(quarters * steps)
    mid = unit_root(quarters * (8.0 * steps))
    wide = unit_root(quarters * (64.0 * steps))
    real_parts, imag_parts = [], []
    for q in range(SG // 64):
        wr, wi = wide[0][q : q + 1], wide[1][q : q + 1]
        real_parts.append(mid[0] * wr - mid[1] * wi)
        imag_parts.append(mid[0] * wi + mid[1] * wr)
    return (jnp.concatenate(real_parts), jnp.concatenate(imag_parts)), fine


def degrid_kernel(grid_ref, dft_ref, rows_ref, out_ref, image_ref):
    @pl.when(pl.program_id(0) == 0)
    def _():
        image_real, image_imag = subgrid_image(
            grid_ref[:, :SG].astype(jnp.bfloat16),
            grid_ref[:, SG:].astype(jnp.bfloat16),
            dft_ref[:, :SG],
            dft_ref[:, SG:],
        )
        image_ref[:SG, :SG] = image_real
        image_ref[:SG, SG:] = -image_imag
        image_ref[SG:, :SG] = image_imag
        image_ref[SG:, SG:] = image_real

    me = lax.axis_index("sub").astype(jnp.float32)

    def one_chunk(index, unused):
        here = pl.ds(pl.multiple_of(index * CHUNK, CHUNK), CHUNK)
        match = rows_ref[0, 0:1, here] == me
        hit = jnp.max(match.astype(jnp.float32)) > 0.0

        @pl.when(hit)
        def _():
            coarse_u, fine_u = powers(rows_ref[0, 1:2, here], CHUNK)
            along_real, along_imag = outer_product(coarse_u, fine_u)
            along = jnp.concatenate(
                [along_real.astype(jnp.bfloat16), along_imag.astype(jnp.bfloat16)]
            )
            inner = plain_dot(image_ref[...], along)
            coarse_v, fine_v = powers(rows_ref[0, 2:3, here], CHUNK)
            ir = inner[:SG].reshape(SG // 8, 8, CHUNK)
            ii = inner[SG:].reshape(SG // 8, 8, CHUNK)
            cr, ci = coarse_v[0][:, None, :], coarse_v[1][:, None, :]
            sum_real = jnp.sum(ir * cr - ii * ci, axis=0)
            sum_imag = jnp.sum(ir * ci + ii * cr, axis=0)
            vis_real = jnp.sum(sum_real * fine_v[0] - sum_imag * fine_v[1], axis=0, keepdims=True)
            vis_imag = jnp.sum(sum_real * fine_v[1] + sum_imag * fine_v[0], axis=0, keepdims=True)
            out_ref[0, :, here] = jnp.where(
                match, jnp.concatenate([vis_real, vis_imag]), 0.0
            )

        @pl.when(jnp.logical_not(hit))
        def _():
            out_ref[0, :, here] = jnp.zeros((2, CHUNK), jnp.float32)

        return unused

    lax.fori_loop(0, rows_ref.shape[2] // CHUNK, one_chunk, 0)


def dft_table():
    spots = np.arange(SG)
    angle = 2.0 * np.pi / SG * (spots[:, None] * spots[None, :] % SG)
    both = np.concatenate([np.cos(angle), np.sin(angle)], axis=1)
    return both.astype(np.float32).astype(jnp.bfloat16)


def local(facet_image, facet_tile, subgrid_cell, row_subgrid, row_uv, observed):
    owners = lax.axis_size("sub")
    rows = row_subgrid.shape[0]
    facet = lax.all_gather(facet_image[0], "sub", axis=0, tiled=True)
    meta = jnp.concatenate([row_subgrid.astype(jnp.float32)[None, :], row_uv], axis=0)
    meta_all = lax.all_gather(meta, "sub", axis=0)
    vmem = pl.BlockSpec(memory_space=pltpu.VMEM)
    smem = pl.BlockSpec(memory_space=pltpu.SMEM)
    terms = pl.pallas_call(
        facet_kernel,
        out_shape=jax.ShapeDtypeStruct((SG, 2 * SG), jnp.float32),
        in_specs=[smem, smem, vmem],
        out_specs=vmem,
        scratch_shapes=[
            pltpu.VMEM((2 * SG, FACET), jnp.bfloat16),
            pltpu.VMEM((2 * SG, FACET), jnp.bfloat16),
        ],
        name="facet_terms",
    )(facet_tile, subgrid_cell, facet)
    grid = lax.psum(terms, "freq")
    partial = pl.pallas_call(
        degrid_kernel,
        grid=(owners,),
        out_shape=jax.ShapeDtypeStruct((owners, 2, rows), jnp.float32),
        in_specs=[
            pl.BlockSpec((SG, 2 * SG), lambda i: (0, 0)),
            pl.BlockSpec((SG, 2 * SG), lambda i: (0, 0)),
            pl.BlockSpec((1, 3, rows), lambda i: (i, 0, 0)),
        ],
        out_specs=pl.BlockSpec((1, 2, rows), lambda i: (i, 0, 0)),
        scratch_shapes=[pltpu.VMEM((2 * SG, 2 * SG), jnp.bfloat16)],
        name="degrid_blocks",
    )(grid, jnp.asarray(dft_table()), meta_all)
    parts = lax.all_to_all(partial, "sub", split_axis=0, concat_axis=0, tiled=True)
    return observed - jnp.sum(parts, axis=0)


def solution(mesh):
    placed = (
        P("freq", "sub", None),
        P("freq", None),
        P("sub", None),
        P(("sub", "freq")),
        P(None, ("sub", "freq")),
        P(None, ("sub", "freq")),
    )
    return jax.shard_map(
        local, mesh=mesh, in_specs=placed, out_specs=P(None, ("sub", "freq")), check_vma=False
    )
```

time: 416 us -> 167 us (0.40)
  the two profiles are of different devices: /device:TPU:8 before, /device:TPU:0 now
where the time goes in v1:
time: 167 us; the launch traced here: 164 us
  waiting for transfers between devices  67 us (40%)
  blocking collectives  53.3 us (32%)
  Pallas kernels  29.7 us (18%)
  between operations  13.4 us (8%)
    all_gather x1, waiting for transfers between devices, local(): facet = lax.all_gather(facet_image[0], 'sub', axis=0, tiled=True)  66.3 us
    all_gather x1, blocking collectives, local(): meta_all = lax.all_gather(meta, 'sub', axis=0)  42.1 us
    pallas_call x1, Pallas kernels, local(): pl.pallas_call(degrid_kernel, grid=(owners,), out_shape=jax.ShapeDtypeStr...  24.9 us
    all_to_all x1, blocking collectives, local(): lax.all_to_all(partial, 'sub', split_axis=0, concat_axis=0, tiled=True)  11.3 us
    pallas_call x1, Pallas kernels, local(): pl.pallas_call(facet_kernel, out_shape=jax.ShapeDtypeStruct((SG, 2 * SG),...  4.77 us
  transfers between devices with their start and end apart: 2, of which 1 were waited for; matrix products, arithmetic and copies ran while one was open for 0% of the time, Pallas kernels for 0%

profile of v1, /device:TPU:0, one launch (start us, length us, event | category | flops | bytes accessed | tf_op | source)
XLA Modules:
  0.0 164.2 jit_solution(8257761329827715252)
XLA Ops:
  6.5 0.0 copy-start.2
  6.5 0.0 copy-start
  6.5 0.0 all-gather.5.cloned.1.call-start
  6.5 0.7 all-gather.5.cloned.1.call-update
  7.3 0.0 all-reduce.2.cloned.1.call-start
  7.3 66.3 %all-gather.5.cloned.1.call-done = bf16[1,1024,1024]{2,1,0:T(8,128)(2,1)} async-done(((bf16[1,64,1024]{2,1,0:T(8,128)(2,1)}), bf16[1,1024,1024]{2,1,0:T(8,128)(2,1)}) %all-gather.5.cloned.1.call-update) | async-done | bytes 2097168 | tf_op jit(solution)/shard_map/all_gather | solution.py:180
  73.6 0.0 copy-start.1
  73.6 4.8 %facet_terms.1 = f32[256,512]{1,0:T(8,128)} custom-call(s32[1,2]{1,0:T(1,128)} %tile_ref.1, s32[1,2]{1,0:T(1,128)} %cell_ref.1, bf16[1024,1024]{1,0:T(8,128)(2,1)} %bitcast.4), custom_call_target="tpu_custom_call" | custom-call | tf_op jit(solution)/shard_map/facet_terms/pallas_call | solution.py:185
  78.3 0.0 all-reduce.2.cloned.1.call-update
  78.4 0.0 copy-done.2
  78.4 0.0 copy-done
  78.4 42.1 %all-gather.2.rows_ref = f32[16,3,1024]{2,1,0:T(4,128)} all-gather(f32[1,3,1024]{2,1,0:T(4,128)S(1)} %maximum_bitcast_fusion), channel_id=3, replica_groups=mesh['sub'=16,'freq'=2] {'sub'}, dimensions={0}, use_global_device_ids=true | all-gather | bytes 208896 | tf_op jit(solution)/shard_map/all_gather | solution.py:182
  120.5 0.0 all-reduce.2.cloned.1.call-done.grid_ref
  120.5 24.9 %degrid_blocks.1 = f32[16,2,1024]{2,1,0:T(2,128)} custom-call(f32[256,512]{1,0:T(8,128)} %all-reduce.2.cloned.1.call-done.grid_ref, bf16[256,512]{1,0:T(8,128)(2,1)} %constant.4.clone.dft_ref, f32[16,3,1024]{2,1,0:T(4,128)} %all-gather.2.rows_ref), custom_call_target="tpu_custom_call" | custom-call | tf_op jit(solution)/shard_map/degrid_blocks/pallas_call | solution.py:197
  145.4 11.3 %all_to_all.5 = f32[16,2,1024]{2,1,0:T(2,128)S(1)} all-to-all(f32[16,2,1024]{2,1,0:T(2,128)} %degrid_blocks.1), channel_id=1, replica_groups=mesh['sub'=16,'freq'=2] {'sub'}, dimensions={0} | all-to-all | bytes 262144 | tf_op jit(solution)/shard_map/all_to_all | solution.py:210
  156.7 0.1 reduce_sum.9
  156.7 0.0 copy-done.1
  156.7 0.6 sub.3
  (2 shorter events, 0.0 us)
Async XLA Ops:
  6.5 71.8 %copy-start.2 = (s32[1024]{0:T(1024)S(1)}, s32[1024]{0:T(1024)}, u32[]{:S(2)}) copy-start(s32[1024]{0:T(1024)} %param.10) | copy-start | bytes 12292
  6.5 71.9 %copy-start = (f32[2,1024]{1,0:T(2,128)S(1)}, f32[2,1024]{1,0:T(2,128)}, u32[]{:S(2)}) copy-start(f32[2,1024]{1,0:T(2,128)} %param.11) | copy-start | bytes 24580
  6.5 67.0 %all-gather.5.cloned.1.call-start = ((), (), s32[]{:S(2)}) async-start(), calls=%async_computation.2 | async-start | bytes 2228224 | tf_op jit(solution)/shard_map/all_gather | solution.py:180
  7.3 113.2 %all-reduce.2.cloned.1.call-start = ((), (), s32[]{:S(2)}) async-start(), calls=%async_computation.1 | async-start | bytes 1048576 | tf_op jit(solution)/shard_map/psum | solution.py:196
  73.6 83.2 %copy-start.1 = (f32[2,1024]{1,0:T(2,128)S(1)}, f32[2,1024]{1,0:T(2,128)}, u32[]{:S(2)}) copy-start(f32[2,1024]{1,0:T(2,128)} %param.12) | copy-start | bytes 24580
Sparse Core Ops, SparseCore 0:
  10.1 63.3 all-gather.4
  78.5 17.3 all-reduce.1

commit v2 on v1

--- a/solution.py
+++ b/solution.py
@@ -1,3 +1,4 @@
+import functools
 import math
 
 import numpy as np
@@ -120,9 +121,10 @@
 def degrid_kernel(grid_ref, dft_ref, rows_ref, out_ref, image_ref):
     @pl.when(pl.program_id(0) == 0)
     def _():
+        grid_sum = jnp.sum(grid_ref[...], axis=0)
         image_real, image_imag = subgrid_image(
-            grid_ref[:, :SG].astype(jnp.bfloat16),
-            grid_ref[:, SG:].astype(jnp.bfloat16),
+            grid_sum[:, :SG].astype(jnp.bfloat16),
+            grid_sum[:, SG:].astype(jnp.bfloat16),
             dft_ref[:, :SG],
             dft_ref[:, SG:],
         )
@@ -174,14 +176,249 @@
     return both.astype(np.float32).astype(jnp.bfloat16)
 
 
+MESH = pl.DeviceIdType.MESH
+PIECES = 3
+
+
+def gather_kernel(layers, facet_ref, meta_ref, facets_ref, metas_ref, send_sem, recv_sem, own_sem):
+    me = lax.axis_index("sub")
+    layer = me // 4
+    in_layer = me % 4
+    pair_y = me - in_layer + (in_layer + 2) % 4
+    pair_x = me + 1 - 2 * (me % 2)
+    diagonal = me - in_layer + (3 - in_layer)
+    above, below = me + 4, me - 4
+    has_above = layer < layers - 1
+    has_below = layer > 0
+    columns = facet_ref.shape[1] // 2
+
+    barrier = pltpu.get_barrier_semaphore()
+    for peer in (pair_y, pair_x):
+        pl.semaphore_signal(barrier, inc=1, device_id={"sub": peer}, device_id_type=MESH)
+
+    @pl.when(has_above)
+    def _():
+        pl.semaphore_signal(barrier, inc=1, device_id={"sub": above}, device_id_type=MESH)
+
+    @pl.when(has_below)
+    def _():
+        pl.semaphore_signal(barrier, inc=1, device_id={"sub": below}, device_id_type=MESH)
+
+    peers = 2 + jnp.minimum(layers - 1 - layer, 1) + jnp.minimum(layer, 1)
+    pl.semaphore_wait(barrier, peers)
+
+    def slot(part, index):
+        if part == 2:
+            return metas_ref.at[index]
+        return facets_ref.at[index, :, part * columns : (part + 1) * columns]
+
+    def own(part):
+        if part == 2:
+            return meta_ref
+        return facet_ref.at[:, part * columns : (part + 1) * columns]
+
+    def copy(part, index, kind, peer, first=False):
+        return pltpu.make_async_remote_copy(
+            src_ref=own(part) if first else slot(part, index),
+            dst_ref=slot(part, index),
+            send_sem=send_sem.at[kind, part, index],
+            recv_sem=recv_sem.at[part, index],
+            device_id={"sub": peer},
+            device_id_type=MESH,
+        )
+
+    def arrived(part, index):
+        copy(part, index, 0, pair_y).wait_recv()
+
+    firsts = [(2, pair_y), (3, pair_x)]
+    seconds = [(3, pair_x), (2, pair_y), (3, pair_x)]
+    partners = [pair_y, pair_x, pair_y]
+    others = [pair_x, pair_y, pair_x]
+
+    def distances(run):
+        for far in range(1, layers):
+
+            @pl.when(layer >= far)
+            def _():
+                run(far, -1)
+
+            @pl.when(layer + far < layers)
+            def _():
+                run(far, 1)
+
+    def onward(act, far, sign):
+        index = me + 4 * far * sign
+
+        @pl.when(has_above if sign < 0 else has_below)
+        def _():
+            for part in range(PIECES):
+                act(copy(part, index, 0 if sign < 0 else 1, above if sign < 0 else below))
+
+    start = lambda c: c.start()
+    wait_send = lambda c: c.wait_send()
+
+    def line_own(act):
+        for part in range(PIECES):
+            for kind, peer in firsts:
+                act(copy(part, me, kind, peer, True))
+
+        @pl.when(has_above)
+        def _():
+            for part in range(PIECES):
+                act(copy(part, me, 0, above, True))
+
+        @pl.when(has_below)
+        def _():
+            for part in range(PIECES):
+                act(copy(part, me, 1, below, True))
+
+    line_own(start)
+    own_facet = pltpu.make_async_copy(facet_ref, facets_ref.at[me], own_sem.at[0])
+    own_meta = pltpu.make_async_copy(meta_ref, metas_ref.at[me], own_sem.at[1])
+    own_facet.start()
+    own_meta.start()
+
+    def second_leg(offset):
+        for part in range(PIECES):
+            index = partners[part] + offset
+            arrived(part, index)
+            copy(part, index, seconds[part][0], seconds[part][1]).start()
+
+    def at_distance(far, act):
+        @pl.when(layer >= far)
+        def _():
+            act(far, -1)
+
+        @pl.when(layer + far < layers)
+        def _():
+            act(far, 1)
+
+    def first_leg(far, sign):
+        index = me + 4 * far * sign
+        for part in range(PIECES):
+            arrived(part, index)
+        onward(start, far, sign)
+        for part in range(PIECES):
+            for kind, peer in firsts:
+                copy(part, index, kind, peer).start()
+
+    for far in range(1, layers):
+        at_distance(far, first_leg)
+        if far == 1:
+            second_leg(0)
+        else:
+            at_distance(far - 1, lambda f, sign: second_leg(4 * f * sign))
+    at_distance(layers - 1, lambda f, sign: second_leg(4 * f * sign))
+
+    def last_leg(offset):
+        for part in range(PIECES):
+            arrived(part, others[part] + offset)
+            arrived(part, diagonal + offset)
+
+    last_leg(0)
+    distances(lambda far, sign: last_leg(4 * far * sign))
+
+    line_own(wait_send)
+    for part in range(PIECES):
+        copy(part, partners[part], seconds[part][0], seconds[part][1]).wait_send()
+
+    def drain(far, sign):
+        onward(wait_send, far, sign)
+        for part in range(PIECES):
+            for kind, peer in firsts:
+                copy(part, me + 4 * far * sign, kind, peer).wait_send()
+            copy(
+                part, partners[part] + 4 * far * sign, seconds[part][0], seconds[part][1]
+            ).wait_send()
+
+    distances(drain)
+    own_facet.wait()
+    own_meta.wait()
+
+
+def scatter_kernel(axis, count, same, parts_ref, out_ref, send_sem, recv_sem, own_sem):
+    me = lax.axis_index(axis)
+    barrier = pltpu.get_barrier_semaphore()
+    for step in range(1, count):
+        peer = lax.rem(me + step, count)
+        pl.semaphore_signal(barrier, inc=1, device_id={axis: peer}, device_id_type=MESH)
+    pl.semaphore_wait(barrier, count - 1)
+
+    def copy(step):
+        peer = lax.rem(me + step, count)
+        return pltpu.make_async_remote_copy(
+            src_ref=parts_ref if same else parts_ref.at[peer],
+            dst_ref=out_ref.at[me],
+            send_sem=send_sem.at[step],
+            recv_sem=recv_sem.at[step],
+            device_id={axis: peer},
+            device_id_type=MESH,
+        )
+
+    for step in range(1, count):
+        copy(step).start()
+    local_copy = pltpu.make_async_copy(
+        parts_ref if same else parts_ref.at[me], out_ref.at[me], own_sem.at[0]
+    )
+    local_copy.start()
+    local_copy.wait()
+    for step in range(1, count):
+        source = lax.rem(me - step + count, count)
+        pltpu.make_async_remote_copy(
+            src_ref=parts_ref if same else parts_ref.at[source],
+            dst_ref=out_ref.at[source],
+            send_sem=send_sem.at[step],
+            recv_sem=recv_sem.at[step],
+            device_id={axis: source},
+            device_id_type=MESH,
+        ).wait_recv()
+    for step in range(1, count):
+        copy(step).wait_send()
+
+
+def direct_scatter(parts, axis, same, collective_id, name):
+    count = lax.axis_size(axis)
+    vmem = pl.BlockSpec(memory_space=pltpu.VMEM)
+    tail = parts.shape if same else parts.shape[1:]
+    return pl.pallas_call(
+        functools.partial(scatter_kernel, axis, count, same),
+        out_shape=jax.ShapeDtypeStruct((count,) + tail, parts.dtype),
+        in_specs=[vmem],
+        out_specs=vmem,
+        scratch_shapes=[
+            pltpu.SemaphoreType.DMA((count,)),
+            pltpu.SemaphoreType.DMA((count,)),
+            pltpu.SemaphoreType.DMA((1,)),
+        ],
+        compiler_params=pltpu.CompilerParams(collective_id=collective_id, has_side_effects=True),
+        name=name,
+    )(parts)
+
+
 def local(facet_image, facet_tile, subgrid_cell, row_subgrid, row_uv, observed):
     owners = lax.axis_size("sub")
     rows = row_subgrid.shape[0]
-    facet = lax.all_gather(facet_image[0], "sub", axis=0, tiled=True)
-    meta = jnp.concatenate([row_subgrid.astype(jnp.float32)[None, :], row_uv], axis=0)
-    meta_all = lax.all_gather(meta, "sub", axis=0)
     vmem = pl.BlockSpec(memory_space=pltpu.VMEM)
     smem = pl.BlockSpec(memory_space=pltpu.SMEM)
+    meta = jnp.concatenate([row_subgrid.astype(jnp.float32)[None, :], row_uv], axis=0)
+    facet_shape = facet_image.shape[1:]
+    facet, meta_all = pl.pallas_call(
+        functools.partial(gather_kernel, owners // 4),
+        out_shape=(
+            jax.ShapeDtypeStruct((owners,) + facet_shape, facet_image.dtype),
+            jax.ShapeDtypeStruct((owners,) + meta.shape, meta.dtype),
+        ),
+        in_specs=[vmem, vmem],
+        out_specs=(vmem, vmem),
+        scratch_shapes=[
+            pltpu.SemaphoreType.DMA((4, PIECES, owners)),
+            pltpu.SemaphoreType.DMA((PIECES, owners)),
+            pltpu.SemaphoreType.DMA((2,)),
+        ],
+        compiler_params=pltpu.CompilerParams(collective_id=0, has_side_effects=True),
+        name="gather_rows",
+    )(facet_image[0], meta)
+    facet = facet.reshape(FACET, FACET)
     terms = pl.pallas_call(
         facet_kernel,
         out_shape=jax.ShapeDtypeStruct((SG, 2 * SG), jnp.float32),
@@ -193,21 +430,21 @@
         ],
         name="facet_terms",
     )(facet_tile, subgrid_cell, facet)
-    grid = lax.psum(terms, "freq")
+    both = direct_scatter(terms, "freq", True, 1, "facet_sum")
     partial = pl.pallas_call(
         degrid_kernel,
         grid=(owners,),
         out_shape=jax.ShapeDtypeStruct((owners, 2, rows), jnp.float32),
         in_specs=[
-            pl.BlockSpec((SG, 2 * SG), lambda i: (0, 0)),
+            pl.BlockSpec(both.shape, lambda i: (0, 0, 0)),
             pl.BlockSpec((SG, 2 * SG), lambda i: (0, 0)),
             pl.BlockSpec((1, 3, rows), lambda i: (i, 0, 0)),
         ],
         out_specs=pl.BlockSpec((1, 2, rows), lambda i: (i, 0, 0)),
         scratch_shapes=[pltpu.VMEM((2 * SG, 2 * SG), jnp.bfloat16)],
         name="degrid_blocks",
-    )(grid, jnp.asarray(dft_table()), meta_all)
-    parts = lax.all_to_all(partial, "sub", split_axis=0, concat_axis=0, tiled=True)
+    )(both, jnp.asarray(dft_table()), meta_all)
+    parts = direct_scatter(partial, "sub", False, 2, "return_rows")
     return observed - jnp.sum(parts, axis=0)
 
 

time: 167 us -> 87 us (0.52); the launches traced: 164 us -> 86.7 us
  waiting for transfers between devices: 67 us -> 0 us
  Pallas kernels: 29.7 us -> 83.1 us
  blocking collectives: 53.3 us -> 0 us
  between operations: 13.4 us -> 0.03 us
  other arithmetic: 0.68 us -> 3.55 us
    all_gather x1 -> x0, waiting for transfers between devices: 66.3 us -> none  [local(): facet = lax.all_gather(facet_image[0], 'sub', axis=0, tiled=True)]
    pallas_call x0 -> x3, Pallas kernels: none -> 58.7 us  [the longest x1 32.2 us: local(): pl.pallas_call(functools.partial(gather_kernel, owners // 4), out_shape=(...]
    all_gather x1 -> x0, blocking collectives: 42.1 us -> none  [local(): meta_all = lax.all_gather(meta, 'sub', axis=0)]
    all_to_all x1 -> x0, blocking collectives: 11.3 us -> none  [local(): lax.all_to_all(partial, 'sub', split_axis=0, concat_axis=0, tiled=True)]
    pallas_call x1, Pallas kernels: 24.9 us -> 19.6 us  [local(): pl.pallas_call(degrid_kernel, grid=(owners,), out_shape=jax.ShapeDtypeStr...]
  transfers between devices with their start and end apart: 2 -> 0, of which waited for: 1 -> 0; matrix products, arithmetic and copies ran while one was open for 0% -> 0% of each run, Pallas kernels for 0% -> 0%
where the time goes in v2:
time: 87 us; the launch traced here: 86.7 us
  Pallas kernels  83.1 us (96%)
  other arithmetic  3.55 us (4%)
    pallas_call x1, Pallas kernels, local(): pl.pallas_call(functools.partial(gather_kernel, owners // 4), out_shape=(...  32.2 us
    pallas_call x2, Pallas kernels, direct_scatter(): pl.pallas_call(functools.partial(scatter_kernel, axis, count, same), out_...  26.5 us
    pallas_call x1, Pallas kernels, local(): pl.pallas_call(degrid_kernel, grid=(owners,), out_shape=jax.ShapeDtypeStr...  19.6 us
    pallas_call x1, Pallas kernels, local(): pl.pallas_call(facet_kernel, out_shape=jax.ShapeDtypeStruct((SG, 2 * SG),...  4.76 us

profile of v2, /device:TPU:0, one launch (start us, length us, event | category | flops | bytes accessed | tf_op | source)
XLA Modules:
  0.0 86.7 jit_solution(10852421847310844917)
XLA Ops:
  0.0 0.7 convert_element_type.3
  0.7 1.3 %pad_maximum_fusion.meta_ref = f32[3,1024]{1,0:T(4,128)} fusion(f32[2,1024]{1,0:T(2,128)} %param.11, f32[1,1024]{1,0:T(1,128)S(1)} %bitcast.5), kind=kLoop, calls=%fused_computation | loop fusion | flops 3072 | bytes 24576 | tf_op jit(solution)/shard_map/concatenate | solution.py:403
  2.0 32.2 %gather_rows.1 = (bf16[16,64,1024]{2,1,0:T(8,128)(2,1)}, f32[16,3,1024]{2,1,0:T(4,128)}) custom-call(bf16[64,1024]{1,0:T(8,128)(2,1)} %bitcast.4, f32[3,1024]{1,0:T(4,128)} %pad_maximum_fusion.meta_ref), custom_call_target="tpu_custom_call" | custom-call | tf_op jit(solution)/shard_map/gather_rows/pallas_call | solution.py:405
  34.2 4.8 %facet_terms.1.parts_ref = f32[256,512]{1,0:T(8,128)} custom-call(s32[1,2]{1,0:T(1,128)} %tile_ref.1, s32[1,2]{1,0:T(1,128)} %cell_ref.1, bf16[1024,1024]{1,0:T(8,128)(2,1)} %bitcast.3), custom_call_target="tpu_custom_call" | custom-call | tf_op jit(solution)/shard_map/facet_terms/pallas_call | solution.py:422
  39.0 0.0 copy-start
  39.0 4.0 %facet_sum.1.grid_ref = f32[2,256,512]{2,1,0:T(8,128)} custom-call(f32[256,512]{1,0:T(8,128)} %facet_terms.1.parts_ref), custom_call_target="tpu_custom_call" | custom-call | tf_op jit(solution)/shard_map/facet_sum/pallas_call | solution.py:383
  43.0 19.6 %degrid_blocks.1.parts_ref = f32[16,2,1024]{2,1,0:T(2,128)} custom-call(f32[2,256,512]{2,1,0:T(8,128)} %facet_sum.1.grid_ref, bf16[256,512]{1,0:T(8,128)(2,1)} %constant.4.clone.dft_ref, f32[16,3,1024]{2,1,0:T(4,128)} %get-tuple-element.8.rows_ref), custom_call_target="tpu_custom_call" | custom-call | tf_op jit(solution)/shard_map/degrid_blocks/pallas_call | solution.py:434
  62.6 22.5 %return_rows.1 = f32[16,2,1024]{2,1,0:T(2,128)} custom-call(f32[16,2,1024]{2,1,0:T(2,128)} %degrid_blocks.1.parts_ref), custom_call_target="tpu_custom_call" | custom-call | tf_op jit(solution)/shard_map/return_rows/pallas_call | solution.py:383
  85.1 1.0 %reduce_sum.9 = f32[2,1024]{1,0:T(2,128)S(1)} reduce(f32[16,2,1024]{2,1,0:T(2,128)} %return_rows.1, f32[]{:T(128)} %constant.1.clone.1), dimensions={0}, to_apply=%region_0.0 | reduce | flops 30720 | bytes 139268 | tf_op jit(solution)/shard_map/reduce_sum | solution.py:448
  86.1 0.0 copy-done
  86.1 0.6 sub.3
Async XLA Ops:
  39.0 47.1 %copy-start = (f32[2,1024]{1,0:T(2,128)S(1)}, f32[2,1024]{1,0:T(2,128)}, u32[]{:S(2)}) copy-start(f32[2,1024]{1,0:T(2,128)} %param.12) | copy-start | bytes 24580

commit v3 on v2

--- a/solution.py
+++ b/solution.py
@@ -104,12 +104,22 @@
     return image_real, image_imag
 
 
+def eighth_power(root):
+    real_part, imag_part = root
+    for _ in range(3):
+        real_part, imag_part = (
+            real_part * real_part - imag_part * imag_part,
+            2.0 * real_part * imag_part,
+        )
+    return real_part, imag_part
+
+
 def powers(position, lanes):
     quarters = position * (4.0 / SG)
     steps = lax.broadcasted_iota(jnp.int32, (8, lanes), 0).astype(jnp.float32)
     fine = unit_root(quarters * steps)
-    mid = unit_root(quarters * (8.0 * steps))
-    wide = unit_root(quarters * (64.0 * steps))
+    mid = eighth_power(fine)
+    wide = eighth_power(mid)
     real_parts, imag_parts = [], []
     for q in range(SG // 64):
         wr, wi = wide[0][q : q + 1], wide[1][q : q + 1]
@@ -118,37 +128,71 @@
     return (jnp.concatenate(real_parts), jnp.concatenate(imag_parts)), fine
 
 
-def degrid_kernel(grid_ref, dft_ref, rows_ref, out_ref, image_ref):
-    @pl.when(pl.program_id(0) == 0)
-    def _():
-        grid_sum = jnp.sum(grid_ref[...], axis=0)
-        image_real, image_imag = subgrid_image(
-            grid_sum[:, :SG].astype(jnp.bfloat16),
-            grid_sum[:, SG:].astype(jnp.bfloat16),
-            dft_ref[:, :SG],
-            dft_ref[:, SG:],
-        )
-        image_ref[:SG, :SG] = image_real
-        image_ref[:SG, SG:] = -image_imag
-        image_ref[SG:, :SG] = image_imag
-        image_ref[SG:, SG:] = image_real
+def permutation(rank):
+    count = rank.shape[1]
+    places = lax.broadcasted_iota(jnp.int32, (count, count), 0).astype(jnp.float32)
+    return jnp.where(places == rank, 1.0, 0.0).astype(jnp.bfloat16)
+
+
+def exact_move(values, product):
+    high = values.astype(jnp.bfloat16)
+    rest = values - high.astype(jnp.float32)
+    mid = rest.astype(jnp.bfloat16)
+    low = (rest - mid.astype(jnp.float32)).astype(jnp.bfloat16)
+    return (product(high) + product(mid)) + product(low)
+
+
+def sort_kernel(labels_ref, uv_ref, meta_ref, rank_ref):
+    labels = labels_ref[...].astype(jnp.float32)
+    count = labels.shape[1]
+    spots = lax.broadcasted_iota(jnp.int32, (1, count), 1).astype(jnp.float32)
+    keys = labels * count + spots
+    turned = jnp.transpose(jnp.broadcast_to(keys, (128, count)))[:, 0:1]
+    rank = jnp.sum(jnp.where(turned < keys, 1.0, 0.0), axis=0, keepdims=True)
+    rank_ref[...] = rank
+    chosen = permutation(rank)
+    values = jnp.concatenate([labels, uv_ref[...], jnp.zeros((5, count), jnp.float32)])
+    meta_ref[...] = exact_move(values, lambda part: nt_dot(part, chosen))[:3]
+
+
+def finish_kernel(parts_ref, rank_ref, observed_ref, out_ref):
+    total = jnp.sum(parts_ref[...], axis=0)
+    padded = jnp.concatenate([total, jnp.zeros((6, total.shape[1]), jnp.float32)])
+    chosen = permutation(rank_ref[...])
+    out_ref[...] = observed_ref[...] - exact_move(padded, lambda part: plain_dot(part, chosen))[:2]
+
+
+def degrid_kernel(hit_ref, grid_ref, dft_ref, rows_ref, out_ref, image_ref):
+    out_ref[...] = jnp.zeros_like(out_ref)
+    grid_sum = jnp.sum(grid_ref[...], axis=0)
+    image_real, image_imag = subgrid_image(
+        grid_sum[:, :SG].astype(jnp.bfloat16),
+        grid_sum[:, SG:].astype(jnp.bfloat16),
+        dft_ref[:, :SG],
+        dft_ref[:, SG:],
+    )
+    image_ref[:SG, :SG] = image_real
+    image_ref[:SG, SG:] = -image_imag
+    image_ref[SG:, :SG] = image_imag
+    image_ref[SG:, SG:] = image_real
 
     me = lax.axis_index("sub").astype(jnp.float32)
+    per_block = rows_ref.shape[2] // CHUNK
 
     def one_chunk(index, unused):
-        here = pl.ds(pl.multiple_of(index * CHUNK, CHUNK), CHUNK)
-        match = rows_ref[0, 0:1, here] == me
-        hit = jnp.max(match.astype(jnp.float32)) > 0.0
-
-        @pl.when(hit)
+        block = index // per_block
+        here = pl.ds(pl.multiple_of((index % per_block) * CHUNK, CHUNK), CHUNK)
+
+        @pl.when(hit_ref[index] > 0)
         def _():
-            coarse_u, fine_u = powers(rows_ref[0, 1:2, here], CHUNK)
+            match = rows_ref[block, 0:1, here] == me
+            coarse_u, fine_u = powers(rows_ref[block, 1:2, here], CHUNK)
             along_real, along_imag = outer_product(coarse_u, fine_u)
             along = jnp.concatenate(
                 [along_real.astype(jnp.bfloat16), along_imag.astype(jnp.bfloat16)]
             )
             inner = plain_dot(image_ref[...], along)
-            coarse_v, fine_v = powers(rows_ref[0, 2:3, here], CHUNK)
+            coarse_v, fine_v = powers(rows_ref[block, 2:3, here], CHUNK)
             ir = inner[:SG].reshape(SG // 8, 8, CHUNK)
             ii = inner[SG:].reshape(SG // 8, 8, CHUNK)
             cr, ci = coarse_v[0][:, None, :], coarse_v[1][:, None, :]
@@ -156,17 +200,13 @@
             sum_imag = jnp.sum(ir * ci + ii * cr, axis=0)
             vis_real = jnp.sum(sum_real * fine_v[0] - sum_imag * fine_v[1], axis=0, keepdims=True)
             vis_imag = jnp.sum(sum_real * fine_v[1] + sum_imag * fine_v[0], axis=0, keepdims=True)
-            out_ref[0, :, here] = jnp.where(
+            out_ref[block, :, here] = jnp.where(
                 match, jnp.concatenate([vis_real, vis_imag]), 0.0
             )
 
-        @pl.when(jnp.logical_not(hit))
-        def _():
-            out_ref[0, :, here] = jnp.zeros((2, CHUNK), jnp.float32)
-
         return unused
 
-    lax.fori_loop(0, rows_ref.shape[2] // CHUNK, one_chunk, 0)
+    lax.fori_loop(0, rows_ref.shape[0] * per_block, one_chunk, 0)
 
 
 def dft_table():
@@ -400,7 +440,16 @@
     rows = row_subgrid.shape[0]
     vmem = pl.BlockSpec(memory_space=pltpu.VMEM)
     smem = pl.BlockSpec(memory_space=pltpu.SMEM)
-    meta = jnp.concatenate([row_subgrid.astype(jnp.float32)[None, :], row_uv], axis=0)
+    meta, rank = pl.pallas_call(
+        sort_kernel,
+        out_shape=(
+            jax.ShapeDtypeStruct((3, rows), jnp.float32),
+            jax.ShapeDtypeStruct((1, rows), jnp.float32),
+        ),
+        in_specs=[vmem, vmem],
+        out_specs=(vmem, vmem),
+        name="sort_rows",
+    )(row_subgrid[None, :], row_uv)
     facet_shape = facet_image.shape[1:]
     facet, meta_all = pl.pallas_call(
         functools.partial(gather_kernel, owners // 4),
@@ -431,21 +480,24 @@
         name="facet_terms",
     )(facet_tile, subgrid_cell, facet)
     both = direct_scatter(terms, "freq", True, 1, "facet_sum")
+    here = meta_all[:, 0, :].reshape(-1, CHUNK) == lax.axis_index("sub").astype(jnp.float32)
+    hits = jnp.max(here.astype(jnp.int32), axis=1)
     partial = pl.pallas_call(
         degrid_kernel,
-        grid=(owners,),
         out_shape=jax.ShapeDtypeStruct((owners, 2, rows), jnp.float32),
-        in_specs=[
-            pl.BlockSpec(both.shape, lambda i: (0, 0, 0)),
-            pl.BlockSpec((SG, 2 * SG), lambda i: (0, 0)),
-            pl.BlockSpec((1, 3, rows), lambda i: (i, 0, 0)),
-        ],
-        out_specs=pl.BlockSpec((1, 2, rows), lambda i: (i, 0, 0)),
+        in_specs=[smem, vmem, vmem, vmem],
+        out_specs=vmem,
         scratch_shapes=[pltpu.VMEM((2 * SG, 2 * SG), jnp.bfloat16)],
         name="degrid_blocks",
-    )(both, jnp.asarray(dft_table()), meta_all)
+    )(hits, both, jnp.asarray(dft_table()), meta_all)
     parts = direct_scatter(partial, "sub", False, 2, "return_rows")
-    return observed - jnp.sum(parts, axis=0)
+    return pl.pallas_call(
+        finish_kernel,
+        out_shape=jax.ShapeDtypeStruct((2, rows), jnp.float32),
+        in_specs=[vmem, vmem, vmem],
+        out_specs=vmem,
+        name="residual_rows",
+    )(parts, rank, observed)
 
 
 def solution(mesh):

time: 87 us -> 68 us (0.78)
  Pallas kernels: 83.1 us -> 65.4 us
  other arithmetic: 3.55 us -> 1.76 us
    pallas_call x2, Pallas kernels: 26.5 us -> 16.3 us  [direct_scatter(): pl.pallas_call(functools.partial(scatter_kernel, axis, count, same), out_...]
    pallas_call x1 -> x3, Pallas kernels: 19.6 us -> 12.1 us  [the longest x1 5.87 us: local(): pl.pallas_call(degrid_kernel, out_shape=jax.ShapeDtypeStruct((owners, 2,...]
    concatenate x1 -> x0, other arithmetic: 1.3 us -> none  [local(): jnp.concatenate([row_subgrid.astype(jnp.float32)[None, :], row_uv], axis=0)]
    reduce_sum x1 -> x0, other arithmetic: 0.96 us -> none  [local(): return observed - jnp.sum(parts, axis=0)]
where the time goes in v3:
time: 68 us; the launch traced here: 67.2 us
  Pallas kernels  65.4 us (96%)
  other arithmetic  1.76 us (3%)
    pallas_call x1, Pallas kernels, local(): pl.pallas_call(functools.partial(gather_kernel, owners // 4), out_shape=(...  32.2 us
    pallas_call x2, Pallas kernels, direct_scatter(): pl.pallas_call(functools.partial(scatter_kernel, axis, count, same), out_...  16.3 us
    pallas_call x1, Pallas kernels, local(): pl.pallas_call(degrid_kernel, out_shape=jax.ShapeDtypeStruct((owners, 2,...  5.87 us
    pallas_call x1, Pallas kernels, local(): pl.pallas_call(facet_kernel, out_shape=jax.ShapeDtypeStruct((SG, 2 * SG),...  4.76 us
    pallas_call x1, Pallas kernels, local(): pl.pallas_call(sort_kernel, out_shape=(jax.ShapeDtypeStruct((3, rows), jn...  3.67 us
    pallas_call x1, Pallas kernels, local(): pl.pallas_call(finish_kernel, out_shape=jax.ShapeDtypeStruct((2, rows), j...  2.55 us

profile of v3, /device:TPU:0, one launch (start us, length us, event | category | flops | bytes accessed | tf_op | source)
XLA Modules:
  0.0 67.2 jit_solution(1367134346032409803)
XLA Ops:
  0.0 3.7 %sort_rows.1 = (f32[3,1024]{1,0:T(4,128)}, f32[1,1024]{1,0:T(1,128)}) custom-call(s32[1,1024]{1,0:T(1,128)} %bitcast.5, f32[2,1024]{1,0:T(2,128)} %uv_ref.1), custom_call_target="tpu_custom_call" | custom-call | tf_op jit(solution)/shard_map/sort_rows/pallas_call | solution.py:443
  3.7 32.2 %gather_rows.1 = (bf16[16,64,1024]{2,1,0:T(8,128)(2,1)}, f32[16,3,1024]{2,1,0:T(4,128)}) custom-call(bf16[64,1024]{1,0:T(8,128)(2,1)} %bitcast.4, f32[3,1024]{1,0:T(4,128)} %get-tuple-element.9.meta_ref), custom_call_target="tpu_custom_call" | custom-call | tf_op jit(solution)/shard_map/gather_rows/pallas_call | solution.py:454
  35.9 4.8 %facet_terms.1.parts_ref = f32[256,512]{1,0:T(8,128)} custom-call(s32[1,2]{1,0:T(1,128)} %tile_ref.1, s32[1,2]{1,0:T(1,128)} %cell_ref.1, bf16[1024,1024]{1,0:T(8,128)(2,1)} %bitcast.3), custom_call_target="tpu_custom_call" | custom-call | tf_op jit(solution)/shard_map/facet_terms/pallas_call | solution.py:471
  40.7 1.1 %fusion = s32[16,1024]{1,0:T(8,128)S(1)} fusion(f32[16,3,1024]{2,1,0:T(4,128)} %get-tuple-element.10.rows_ref, f32[]{:T(128)S(6)} %convert_element_type.9), kind=kLoop, calls=%fused_computation.1 | loop fusion | flops 32768 | bytes 131076 | tf_op jit(solution)/shard_map/convert_element_type | solution.py:484
  41.8 0.6 reduce_max.9.hit_ref
  42.5 4.0 %facet_sum.1.grid_ref = f32[2,256,512]{2,1,0:T(8,128)} custom-call(f32[256,512]{1,0:T(8,128)} %facet_terms.1.parts_ref), custom_call_target="tpu_custom_call" | custom-call | tf_op jit(solution)/shard_map/facet_sum/pallas_call | solution.py:423
  46.5 5.9 %degrid_blocks.1.parts_ref = f32[16,2,1024]{2,1,0:T(2,128)} custom-call(s32[64]{0:T(128)} %reduce_max.9.hit_ref, f32[2,256,512]{2,1,0:T(8,128)} %facet_sum.1.grid_ref, bf16[256,512]{1,0:T(8,128)(2,1)} %constant.10.clone.dft_ref, f32[16,3,1024]{2,1,0:T(4,128)} %get-tuple-element.10.rows_ref), custom_call_target="tpu_custom_call" | custom-call | tf_op jit(solution)/shard_map/degrid_blocks/pallas_call | solution.py:485
  52.3 12.3 %return_rows.1.parts_ref = f32[16,2,1024]{2,1,0:T(2,128)} custom-call(f32[16,2,1024]{2,1,0:T(2,128)} %degrid_blocks.1.parts_ref), custom_call_target="tpu_custom_call" | custom-call | tf_op jit(solution)/shard_map/return_rows/pallas_call | solution.py:423
  64.6 2.5 %residual_rows.1 = f32[2,1024]{1,0:T(2,128)} custom-call(f32[16,2,1024]{2,1,0:T(2,128)} %return_rows.1.parts_ref, f32[1,1024]{1,0:T(1,128)} %get-tuple-element.12.rank_ref, f32[2,1024]{1,0:T(2,128)} %observed_ref.1), custom_call_target="tpu_custom_call" | custom-call | tf_op jit(solution)/shard_map/residual_rows/pallas_call | solution.py:494
  (1 shorter events, 0.0 us)

commit v4 on v3

--- a/solution.py
+++ b/solution.py
@@ -69,16 +69,17 @@
     return real_part.astype(jnp.bfloat16), imag_part.astype(jnp.bfloat16)
 
 
-def facet_kernel(tile_ref, cell_ref, image_ref, out_ref, col_ref, spectra_ref):
-    col_real, col_imag = window_table(cell_ref[0, 0], tile_ref[0, 0] * FACET)
-    col_ref[:SG] = col_real
-    col_ref[SG:] = col_imag
+def facet_kernel(table_ref, image_ref, rows_ref, out_ref, hit_ref, spectra_ref):
+    me = lax.axis_index("sub").astype(jnp.float32)
+    here = jnp.where(rows_ref[:, 0, :] == me, 1, 0)
+    for chunk in range(hit_ref.shape[1]):
+        part = here[:, chunk * CHUNK : (chunk + 1) * CHUNK]
+        hit_ref[:, chunk : chunk + 1] = jnp.max(part, axis=1, keepdims=True)
     for part in range(4):
         rows = slice(part * 256, part * 256 + 256)
-        spectra_ref[:, rows] = nt_dot(col_ref[...], image_ref[rows]).astype(jnp.bfloat16)
-    row_real, row_imag = window_table(cell_ref[0, 1], tile_ref[0, 1] * FACET)
-    first = nt_dot(row_real, spectra_ref[...])
-    second = nt_dot(row_imag, spectra_ref[...])
+        spectra_ref[:, rows] = nt_dot(table_ref[: 2 * SG], image_ref[rows]).astype(jnp.bfloat16)
+    first = nt_dot(table_ref[2 * SG : 3 * SG], spectra_ref[...])
+    second = nt_dot(table_ref[3 * SG :], spectra_ref[...])
     out_ref[:, :SG] = first[:, :SG] - second[:, SG:]
     out_ref[:, SG:] = first[:, SG:] + second[:, :SG]
 
@@ -183,7 +184,7 @@
         block = index // per_block
         here = pl.ds(pl.multiple_of((index % per_block) * CHUNK, CHUNK), CHUNK)
 
-        @pl.when(hit_ref[index] > 0)
+        @pl.when(hit_ref[block, index % per_block] > 0)
         def _():
             match = rows_ref[block, 0:1, here] == me
             coarse_u, fine_u = powers(rows_ref[block, 1:2, here], CHUNK)
@@ -220,7 +221,10 @@
 PIECES = 3
 
 
-def gather_kernel(layers, facet_ref, meta_ref, facets_ref, metas_ref, send_sem, recv_sem, own_sem):
+def gather_kernel(
+    layers, tile_ref, cell_ref, facet_ref, meta_ref, facets_ref, metas_ref, table_ref,
+    send_sem, recv_sem, own_sem,
+):
     me = lax.axis_index("sub")
     layer = me // 4
     in_layer = me % 4
@@ -317,6 +321,10 @@
     own_meta = pltpu.make_async_copy(meta_ref, metas_ref.at[me], own_sem.at[1])
     own_facet.start()
     own_meta.start()
+    for axis in range(2):
+        real_part, imag_part = window_table(cell_ref[0, axis], tile_ref[0, axis] * FACET)
+        table_ref[2 * axis * SG : (2 * axis + 1) * SG] = real_part
+        table_ref[(2 * axis + 1) * SG : (2 * axis + 2) * SG] = imag_part
 
     def second_leg(offset):
         for part in range(PIECES):
@@ -451,14 +459,15 @@
         name="sort_rows",
     )(row_subgrid[None, :], row_uv)
     facet_shape = facet_image.shape[1:]
-    facet, meta_all = pl.pallas_call(
+    facet, meta_all, tables = pl.pallas_call(
         functools.partial(gather_kernel, owners // 4),
         out_shape=(
             jax.ShapeDtypeStruct((owners,) + facet_shape, facet_image.dtype),
             jax.ShapeDtypeStruct((owners,) + meta.shape, meta.dtype),
+            jax.ShapeDtypeStruct((4 * SG, FACET), jnp.bfloat16),
         ),
-        in_specs=[vmem, vmem],
-        out_specs=(vmem, vmem),
+        in_specs=[smem, smem, vmem, vmem],
+        out_specs=(vmem, vmem, vmem),
         scratch_shapes=[
             pltpu.SemaphoreType.DMA((4, PIECES, owners)),
             pltpu.SemaphoreType.DMA((PIECES, owners)),
@@ -466,22 +475,22 @@
         ],
         compiler_params=pltpu.CompilerParams(collective_id=0, has_side_effects=True),
         name="gather_rows",
-    )(facet_image[0], meta)
+    )(facet_tile, subgrid_cell, facet_image[0], meta)
     facet = facet.reshape(FACET, FACET)
-    terms = pl.pallas_call(
+    terms, hits = pl.pallas_call(
         facet_kernel,
-        out_shape=jax.ShapeDtypeStruct((SG, 2 * SG), jnp.float32),
-        in_specs=[smem, smem, vmem],
-        out_specs=vmem,
+        out_shape=(
+            jax.ShapeDtypeStruct((SG, 2 * SG), jnp.float32),
+            jax.ShapeDtypeStruct((owners, rows // CHUNK), jnp.int32),
+        ),
+        in_specs=[vmem, vmem, vmem],
+        out_specs=(vmem, vmem),
         scratch_shapes=[
-            pltpu.VMEM((2 * SG, FACET), jnp.bfloat16),
             pltpu.VMEM((2 * SG, FACET), jnp.bfloat16),
         ],
         name="facet_terms",
-    )(facet_tile, subgrid_cell, facet)
+    )(tables, facet, meta_all)
     both = direct_scatter(terms, "freq", True, 1, "facet_sum")
-    here = meta_all[:, 0, :].reshape(-1, CHUNK) == lax.axis_index("sub").astype(jnp.float32)
-    hits = jnp.max(here.astype(jnp.int32), axis=1)
     partial = pl.pallas_call(
         degrid_kernel,
         out_shape=jax.ShapeDtypeStruct((owners, 2, rows), jnp.float32),

time: 68 us -> 66.7 us (0.981); the launches traced: 67.2 us -> 66.6 us
  other arithmetic: 1.76 us -> 0 us
  Pallas kernels: 65.4 us -> 66.6 us
    pallas_call x1, Pallas kernels: 5.87 us -> 7.11 us  [local(): pl.pallas_call(degrid_kernel, out_shape=jax.ShapeDtypeStruct((owners, 2,...]
    convert_element_type x1 -> x0, other arithmetic: 1.13 us -> none  [local(): hits = jnp.max(here.astype(jnp.int32), axis=1)]
    pallas_call x2, Pallas kernels: 16.3 us -> 15.5 us  [direct_scatter(): pl.pallas_call(functools.partial(scatter_kernel, axis, count, same), out_...]
where the time goes in v4:
time: 66.7 us; the launch traced here: 66.6 us
  Pallas kernels  66.6 us (100%)
    pallas_call x1, Pallas kernels, local(): pl.pallas_call(functools.partial(gather_kernel, owners // 4), out_shape=(...  32.9 us
    pallas_call x2, Pallas kernels, direct_scatter(): pl.pallas_call(functools.partial(scatter_kernel, axis, count, same), out_...  15.5 us
    pallas_call x1, Pallas kernels, local(): pl.pallas_call(degrid_kernel, out_shape=jax.ShapeDtypeStruct((owners, 2,...  7.11 us
    pallas_call x1, Pallas kernels, local(): pl.pallas_call(facet_kernel, out_shape=(jax.ShapeDtypeStruct((SG, 2 * SG)...  4.85 us
    pallas_call x1, Pallas kernels, local(): pl.pallas_call(sort_kernel, out_shape=(jax.ShapeDtypeStruct((3, rows), jn...  3.67 us
    pallas_call x1, Pallas kernels, local(): pl.pallas_call(finish_kernel, out_shape=jax.ShapeDtypeStruct((2, rows), j...  2.55 us

profile of v4, /device:TPU:0, one launch (start us, length us, event | category | flops | bytes accessed | tf_op | source)
XLA Modules:
  0.0 66.6 jit_solution(5184559693750653846)
XLA Ops:
  0.0 3.7 %sort_rows.1 = (f32[3,1024]{1,0:T(4,128)}, f32[1,1024]{1,0:T(1,128)}) custom-call(s32[1,1024]{1,0:T(1,128)} %bitcast.5, f32[2,1024]{1,0:T(2,128)} %uv_ref.1), custom_call_target="tpu_custom_call" | custom-call | tf_op jit(solution)/shard_map/sort_rows/pallas_call | solution.py:451
  3.7 32.9 %gather_rows.1 = (bf16[16,64,1024]{2,1,0:T(8,128)(2,1)}, f32[16,3,1024]{2,1,0:T(4,128)}, bf16[1024,1024]{1,0:T(8,128)(2,1)}) custom-call(s32[1,2]{1,0:T(1,128)} %tile_ref.1, s32[1,2]{1,0:T(1,128)} %cell_ref.1, bf16[64,1024]{1,0:T(8,128)(2,1)} %bitcast.4, f32[3,1024]{1,0:T(4,128)} %get-tuple-element.12.meta_ref), custom_call_target="tpu_custom_call" | custom-call | tf_op jit(solution)/shard_map/gather_rows/pallas_call | solution.py:462
  36.5 4.8 %facet_terms.1 = (f32[256,512]{1,0:T(8,128)}, s32[16,4]{1,0:T(8,128)}) custom-call(bf16[1024,1024]{1,0:T(8,128)(2,1)} %get-tuple-element.13.table_ref, bf16[1024,1024]{1,0:T(8,128)(2,1)} %bitcast.3, f32[16,3,1024]{2,1,0:T(4,128)} %get-tuple-element.15.rows_ref), custom_call_target="tpu_custom_call" | custom-call | tf_op jit(solution)/shard_map/facet_terms/pallas_call | solution.py:480
  41.4 4.0 %facet_sum.1.grid_ref = f32[2,256,512]{2,1,0:T(8,128)} custom-call(f32[256,512]{1,0:T(8,128)} %get-tuple-element.17.parts_ref), custom_call_target="tpu_custom_call" | custom-call | tf_op jit(solution)/shard_map/facet_sum/pallas_call | solution.py:431
  45.4 7.1 %degrid_blocks.1.parts_ref = f32[16,2,1024]{2,1,0:T(2,128)} custom-call(s32[16,4]{1,0:T(8,128)} %get-tuple-element.16.hit_ref, f32[2,256,512]{2,1,0:T(8,128)} %facet_sum.1.grid_ref, bf16[256,512]{1,0:T(8,128)(2,1)} %constant.2.clone.dft_ref, f32[16,3,1024]{2,1,0:T(4,128)} %get-tuple-element.15.rows_ref), custom_call_target="tpu_custom_call" | custom-call | tf_op jit(solution)/shard_map/degrid_blocks/pallas_call | solution.py:494
  52.5 11.6 %return_rows.1.parts_ref = f32[16,2,1024]{2,1,0:T(2,128)} custom-call(f32[16,2,1024]{2,1,0:T(2,128)} %degrid_blocks.1.parts_ref), custom_call_target="tpu_custom_call" | custom-call | tf_op jit(solution)/shard_map/return_rows/pallas_call | solution.py:431
  64.1 2.5 %residual_rows.1 = f32[2,1024]{1,0:T(2,128)} custom-call(f32[16,2,1024]{2,1,0:T(2,128)} %return_rows.1.parts_ref, f32[1,1024]{1,0:T(1,128)} %get-tuple-element.18.rank_ref, f32[2,1024]{1,0:T(2,128)} %observed_ref.1), custom_call_target="tpu_custom_call" | custom-call | tf_op jit(solution)/shard_map/residual_rows/pallas_call | solution.py:503

commit v5 on v4

--- a/solution.py
+++ b/solution.py
@@ -12,7 +12,7 @@
 SG = 256
 FACET = 1024
 NIMG = 65536
-CHUNK = 256
+CHUNK = 128
 HALF_PI = math.pi / 2.0
 
 

time: 66.7 us -> 69.7 us (1.045)
  Pallas kernels: 66.6 us -> 69.2 us
    pallas_call x2, Pallas kernels: 15.5 us -> 18.9 us  [direct_scatter(): pl.pallas_call(functools.partial(scatter_kernel, axis, count, same), out_...]
where the time goes in v5:
time: 69.7 us; the launch traced here: 69.3 us
  Pallas kernels  69.2 us (99%)
    pallas_call x1, Pallas kernels, local(): pl.pallas_call(functools.partial(gather_kernel, owners // 4), out_shape=(...  32.9 us
    pallas_call x2, Pallas kernels, direct_scatter(): pl.pallas_call(functools.partial(scatter_kernel, axis, count, same), out_...  18.9 us
    pallas_call x1, Pallas kernels, local(): pl.pallas_call(degrid_kernel, out_shape=jax.ShapeDtypeStruct((owners, 2,...  6.45 us
    pallas_call x1, Pallas kernels, local(): pl.pallas_call(facet_kernel, out_shape=(jax.ShapeDtypeStruct((SG, 2 * SG)...  4.85 us
    pallas_call x1, Pallas kernels, local(): pl.pallas_call(sort_kernel, out_shape=(jax.ShapeDtypeStruct((3, rows), jn...  3.67 us
    pallas_call x1, Pallas kernels, local(): pl.pallas_call(finish_kernel, out_shape=jax.ShapeDtypeStruct((2, rows), j...  2.55 us

profile of v5, /device:TPU:0, one launch (start us, length us, event | category | flops | bytes accessed | tf_op | source)
XLA Modules:
  0.0 69.3 jit_solution(1917174570662269578)
XLA Ops:
  0.0 3.7 %sort_rows.1 = (f32[3,1024]{1,0:T(4,128)}, f32[1,1024]{1,0:T(1,128)}) custom-call(s32[1,1024]{1,0:T(1,128)} %bitcast.5, f32[2,1024]{1,0:T(2,128)} %uv_ref.1), custom_call_target="tpu_custom_call" | custom-call | tf_op jit(solution)/shard_map/sort_rows/pallas_call | solution.py:451
  3.7 32.9 %gather_rows.1 = (bf16[16,64,1024]{2,1,0:T(8,128)(2,1)}, f32[16,3,1024]{2,1,0:T(4,128)}, bf16[1024,1024]{1,0:T(8,128)(2,1)}) custom-call(s32[1,2]{1,0:T(1,128)} %tile_ref.1, s32[1,2]{1,0:T(1,128)} %cell_ref.1, bf16[64,1024]{1,0:T(8,128)(2,1)} %bitcast.4, f32[3,1024]{1,0:T(4,128)} %get-tuple-element.12.meta_ref), custom_call_target="tpu_custom_call" | custom-call | tf_op jit(solution)/shard_map/gather_rows/pallas_call | solution.py:462
  36.5 4.8 %facet_terms.1 = (f32[256,512]{1,0:T(8,128)}, s32[16,8]{1,0:T(8,128)}) custom-call(bf16[1024,1024]{1,0:T(8,128)(2,1)} %get-tuple-element.13.table_ref, bf16[1024,1024]{1,0:T(8,128)(2,1)} %bitcast.3, f32[16,3,1024]{2,1,0:T(4,128)} %get-tuple-element.15.rows_ref), custom_call_target="tpu_custom_call" | custom-call | tf_op jit(solution)/shard_map/facet_terms/pallas_call | solution.py:480
  41.4 4.0 %facet_sum.1.grid_ref = f32[2,256,512]{2,1,0:T(8,128)} custom-call(f32[256,512]{1,0:T(8,128)} %get-tuple-element.17.parts_ref), custom_call_target="tpu_custom_call" | custom-call | tf_op jit(solution)/shard_map/facet_sum/pallas_call | solution.py:431
  45.4 6.4 %degrid_blocks.1.parts_ref = f32[16,2,1024]{2,1,0:T(2,128)} custom-call(s32[16,8]{1,0:T(8,128)} %get-tuple-element.16.hit_ref, f32[2,256,512]{2,1,0:T(8,128)} %facet_sum.1.grid_ref, bf16[256,512]{1,0:T(8,128)(2,1)} %constant.2.clone.dft_ref, f32[16,3,1024]{2,1,0:T(4,128)} %get-tuple-element.15.rows_ref), custom_call_target="tpu_custom_call" | custom-call | tf_op jit(solution)/shard_map/degrid_blocks/pallas_call | solution.py:494
  51.8 14.9 %return_rows.1.parts_ref = f32[16,2,1024]{2,1,0:T(2,128)} custom-call(f32[16,2,1024]{2,1,0:T(2,128)} %degrid_blocks.1.parts_ref), custom_call_target="tpu_custom_call" | custom-call | tf_op jit(solution)/shard_map/return_rows/pallas_call | solution.py:431
  66.7 2.5 %residual_rows.1 = f32[2,1024]{1,0:T(2,128)} custom-call(f32[16,2,1024]{2,1,0:T(2,128)} %return_rows.1.parts_ref, f32[1,1024]{1,0:T(1,128)} %get-tuple-element.18.rank_ref, f32[2,1024]{1,0:T(2,128)} %observed_ref.1), custom_call_target="tpu_custom_call" | custom-call | tf_op jit(solution)/shard_map/residual_rows/pallas_call | solution.py:503
